TPU v7x, 512 devices: a whole 4x8x8 slice. The times are simulated.
512 devices in a mesh: slab: 512 (over z, x, y, core).
Axes of the slice: x: 4, y: 8, z: 8, core: 2. Of those that a mesh axis runs over, the one named last changes fastest.
Arguments:
- krylov_basis_block: float32 [16, 4096, 16, 128], P(None, 'slab'), may hold values from -6 to 6
- companion: float32 [16, 4096, 16, 128], P(None, 'slab'), may hold values from -6 to 6
- region: int32 [4096, 16, 128], P('slab'), may hold values from 0 to 7
- inv_density: float32 [8], replicated, may hold values from 0.3 to 3
- stiffness: float32 [8], replicated, may hold values from 0.5 to 3
- damping: float32 [8], replicated, may hold values from 0.5 to 4
Outputs:
- new_block: float32 [16, 4096, 16, 128], P(None, 'slab')
- projection: float32 [16, 16], replicated
- rfactor: float32 [16, 16], replicated
All inputs are finite; a program needn't handle non-finite values.
Results may differ from a plain program's by a relative error of at most 0.00012.
Values sent between devices are 32-bit elements; how exact they have to be, the bound alone decides.
No kernel may reach another device: no remote copies, remote signals or barrier semaphores. Data moves between devices by JAX's collectives and lax.ppermute only.
A program may use at most 64 MiB of HBM per device.

v0:
```python
import jax
import jax.numpy as jnp
from jax import lax
from jax.sharding import Mesh
from jax.sharding import PartitionSpec as P

SLAB = ("slab_0", "slab_1", "slab_2", "slab_3")


def extended(cells, sides, width):
    for axis, dim in sides:
        count = lax.axis_size(axis)
        ends = count - 1
        head = lax.slice_in_dim(cells, 0, width, axis=dim)
        tail = lax.slice_in_dim(cells, cells.shape[dim] - width, cells.shape[dim], axis=dim)
        cells = jnp.concatenate(
            [
                lax.ppermute(tail, axis, [(i, (i + 1) % count) for i in range(ends)]),
                cells,
                lax.ppermute(head, axis, [((i + 1) % count, i) for i in range(ends)]),
            ],
            axis=dim,
        )
    return cells


def sent_to_all(x, axis):
    peers = lax.axis_size(axis)
    return lax.all_to_all(jnp.broadcast_to(x[None], (peers, *x.shape)), axis, 0, 0, tiled=True)


def taken_together(x, axis):
    return sent_to_all(x, axis).sum(axis=0)


def over_axes(x, axes):
    far, near = axes
    return taken_together(taken_together(x, near), far)


def together(arrays, axis):
    ends = [0]
    for a in arrays:
        ends.append(ends[-1] + a.size)
    running = over_axes(jnp.concatenate([a.ravel() for a in arrays]), axis)
    return tuple((running[b:e].reshape(a.shape) for a, b, e in zip(arrays, ends, ends[1:])))


def lookup(region, table):
    picks = region[None] == jnp.arange(table.shape[0], dtype=jnp.int32)[:, None, None, None]
    return jnp.sum(jnp.where(picks, table[:, None, None, None], jnp.float32(0.0)), axis=0)


def operate(operator_applied, cx, mass, damp, companion):
    padded_basis = jnp.pad(operator_applied, ((0, 0), (0, 0), (1, 1), (1, 1)))
    cpad = jnp.pad(cx, ((0, 0), (1, 1), (1, 1)), mode="edge")
    center_coefficient = padded_basis[:, 1:-1, 1:-1, 1:-1]
    ccenter = cpad[1:-1, 1:-1, 1:-1]
    total = -mass * center_coefficient + damp * companion
    shifts = [
        (slice(2, None), slice(1, -1), slice(1, -1)),
        (slice(0, -2), slice(1, -1), slice(1, -1)),
        (slice(1, -1), slice(2, None), slice(1, -1)),
        (slice(1, -1), slice(0, -2), slice(1, -1)),
        (slice(1, -1), slice(1, -1), slice(2, None)),
        (slice(1, -1), slice(1, -1), slice(0, -2)),
    ]
    for selection_mask in shifts:
        neighbour_coefficient = padded_basis[
            :, selection_mask[0], selection_mask[1], selection_mask[2]
        ]
        bond = 0.5 * (ccenter + cpad[selection_mask])
        total = total + bond * (center_coefficient - neighbour_coefficient)
    return total


def edge_term(center_coefficient, own_coef, other_values, other_coef):
    usable = jnp.where(other_coef > 0.0, other_coef, own_coef)
    return (
        0.5 * (own_coef + usable) * (center_coefficient - other_values)
        - own_coef * center_coefficient
    )


def block_products(left, right):
    return jnp.dot(left, right.T, precision=lax.Precision.HIGHEST)


def shards(krylov_basis_block, companion, region, inv_density, stiffness, damping):
    block_width = krylov_basis_block.shape[0]
    coef = lookup(region, inv_density)
    mass = lookup(region, stiffness)
    damp = lookup(region, damping)
    stacked = jnp.concatenate([krylov_basis_block, coef[None]], axis=0)
    operator_applied = jnp.pad(krylov_basis_block, ((0, 0), (1, 1), (0, 0), (0, 0)))
    cx = jnp.pad(coef, ((1, 1), (0, 0), (0, 0)), mode="edge")
    fresh = operate(operator_applied, cx, mass, damp, companion)
    padded = extended(stacked, ((SLAB, 1),), 1)
    lower_fix = edge_term(
        krylov_basis_block[:, 0], coef[0], padded[:block_width, 0], padded[block_width, 0]
    )
    upper_fix = edge_term(
        krylov_basis_block[:, -1], coef[-1], padded[:block_width, -1], padded[block_width, -1]
    )
    fresh = fresh.at[:, 0].add(lower_fix)
    fresh = fresh.at[:, -1].add(upper_fix)
    cell_count = (
        krylov_basis_block.shape[1]
        * krylov_basis_block.shape[2]
        * krylov_basis_block.shape[3]
        * lax.axis_size(SLAB)
    )
    basis_matrix = krylov_basis_block.reshape(block_width, -1)
    image_matrix = fresh.reshape(block_width, -1)
    projection, fresh_gram, basis_gram = together(
        (
            block_products(basis_matrix, image_matrix) / cell_count,
            block_products(image_matrix, image_matrix) / cell_count,
            block_products(basis_matrix, basis_matrix) / cell_count,
        ),
        ("slab_0", ("slab_1", "slab_2", "slab_3")),
    )
    cross = block_products(projection.T, projection.T)
    spread = jnp.dot(
        projection.T,
        jnp.dot(basis_gram, projection, precision=lax.Precision.HIGHEST),
        precision=lax.Precision.HIGHEST,
    )
    gram = fresh_gram - 2.0 * cross + spread
    lower = jnp.linalg.cholesky(gram)
    reduced_products = image_matrix - jnp.dot(
        projection.T, basis_matrix, precision=lax.Precision.HIGHEST
    )
    new_block = lax.linalg.triangular_solve(lower, reduced_products, left_side=True, lower=True)
    return (new_block.reshape(krylov_basis_block.shape), projection, lower.T)


def solution(mesh):
    torus = Mesh(mesh.devices.reshape(8, 4, 8, 2), ("slab_0", "slab_1", "slab_2", "slab_3"))
    placed = (
        P(None, SLAB, None, None),
        P(None, SLAB, None, None),
        P(SLAB, None, None),
        P(),
        P(),
        P(),
    )
    return jax.shard_map(
        shards,
        mesh=torus,
        in_specs=placed,
        out_specs=(P(None, SLAB, None, None), P(), P()),
        check_vma=False,
    )
```

profile of v0, /device:TPU:1, one launch (start us, length us, event | category | flops | bytes accessed | tf_op | source)
XLA Modules:
  0.0 71.0 jit_solution(1586842108517137983)
XLA Ops:
  0.6 0.0 copy-start
  0.6 1.2 %select_reduce_fusion.2 = (f32[8,16,128]{2,1,0:T(8,128)S(1)}, f32[8,16,128]{2,1,0:T(8,128)S(1)}, f32[8,16,128]{2,1,0:T(8,128)S(1)}) fusion(f32[8]{0:T(128)} %param.14, s32[8,16,128]{2,1,0:T(8,128)} %param.12, f32[8]{0:T(128)} %param.13, f32[8]{0:T(128)} %param.15), kind=kLoop, calls=%fused_computation.38 | loop fusion | flops 868352 | bytes 262240 | tf_op jit(solution)/shard_map/reduce_sum | solution.py:51
  1.8 1.0 %pad_maximum_fusion = (f32[17,1,16,128]{3,2,1,0:T(8,128)S(1)}, f32[17,1,16,128]{3,2,1,0:T(8,128)S(1)}) fusion(f32[1,8,16,128]{3,2,1,0:T(8,128)S(1)} %bitcast.78, f32[16,8,16,128]{3,2,1,0:T(8,128)} %param.10), kind=kLoop, calls=%fused_computation.40 | loop fusion | flops 69632 | bytes 1392640 | tf_op jit(solution)/shard_map/concatenate | solution.py:94
  2.8 4.6 %collective-permute-start = (f32[17,1,16,128]{3,2,1,0:T(8,128)S(1)}, f32[17,1,16,128]{3,2,1,0:T(8,128)S(1)}, u32[]{:S(2)}, u32[]{:S(2)}) collective-permute-start(f32[17,1,16,128]{3,2,1,0:T(8,128)S(1)} %get-tuple-element.43), channel_id=1, source_target_pairs={{0,1},{1,2},{2,3},{3,4},{4,5},{5,6},{6,7},{7,8},{8,9},{9,10},{10,1... | collective-permute-start | bytes 417800 | tf_op jit(solution)/shard_map/ppermute | solution.py:18
  7.4 5.5 %collective-permute-start.1 = (f32[17,1,16,128]{3,2,1,0:T(8,128)S(1)}, f32[17,1,16,128]{3,2,1,0:T(8,128)S(1)}, u32[]{:S(2)}, u32[]{:S(2)}) collective-permute-start(f32[17,1,16,128]{3,2,1,0:T(8,128)S(1)} %get-tuple-element.42), channel_id=1, source_target_pairs={{1,0},{2,1},{3,2},{4,3},{5,4},{6,5},{7,6},{8,7},{9,8},{10,9},{11,1... | collective-permute-start | bytes 417800 | tf_op jit(solution)/shard_map/ppermute | solution.py:20
  12.9 0.0 copy-done
  12.9 0.1 pad.12
  13.0 1.8 %fusion.2 = f32[16,16]{1,0:T(8,128)S(1)} fusion(f32[16,8,16,128]{3,2,1,0:T(8,128)S(1)} %copy-done), kind=kOutput, calls=%fused_computation.10 | convolution fusion | flops 50331904 | bytes 1049600 | tf_op jit(solution)/shard_map/dot_general | solution.py:86
  14.9 0.1 reshape.181
  15.0 0.0 collective-permute-done
  15.0 0.0 copy-start.3
  15.0 0.0 collective-permute-done.1
  15.0 0.0 copy-start.1
  15.1 0.6 copy-done.1
  15.7 0.0 copy-done.3
  15.7 0.1 fusion.55
  15.8 0.1 fusion.37
  15.9 0.0 copy-start.4
  16.0 0.0 copy-start.2
  16.0 2.2 %fusion.11 = f32[16,8,16,128]{3,2,1,0:T(8,128)S(1)} fusion(f32[16,8,16,128]{3,2,1,0:T(8,128)S(1)} %copy-done, f32[16,10,16,128]{3,2,1,0:T(8,128)S(1)} %pad.12, f32[16,8,16,128]{3,2,1,0:T(8,128)} %param.11, f32[8,16,128]{2,1,0:T(8,128)S(1)} %get-tuple-element.47, f32[8,16,128]{2,1,0:T(8,128)S(1)} %get-tuple-element.46, ...), kind=kLoop, calls=%fused_computation.21 | loop fusion | flops 5505024 | bytes 7077888 | tf_op jit(solution)/shard_map/add | solution.py:73
  18.2 0.0 copy-done.4
  18.2 0.1 fusion.33
  18.3 0.0 copy-done.2
  18.3 0.1 fusion.29
  18.4 2.5 %fusion.5 = f32[16,16]{0,1:T(8,128)S(1)} fusion(f32[16,8,16,128]{3,2,1,0:T(8,128)S(1)} %copy-done, f32[16,8,16,128]{3,2,1,0:T(8,128)S(1)} %fusion.29), kind=kOutput, calls=%fused_computation.15 | convolution fusion | flops 50331904 | bytes 2098176 | tf_op jit(solution)/shard_map/dot_general | solution.py:86
  20.8 1.9 %fusion.3 = f32[16,16]{1,0:T(8,128)S(1)} fusion(f32[16,8,16,128]{3,2,1,0:T(8,128)S(1)} %fusion.29), kind=kOutput, calls=%fused_computation.12 | convolution fusion | flops 50331904 | bytes 1049600 | tf_op jit(solution)/shard_map/dot_general | solution.py:86
  22.7 0.1 copy.54
  22.8 0.1 reshape.179
  22.8 0.1 reshape.180
  23.0 0.1 broadcast_in_dim.36
  23.1 21.2 %all_to_all.12 = f32[64,1,768]{2,1,0:T(1,128)S(1)} all-to-all(f32[64,1,768]{2,1,0:T(1,128)S(1)} %broadcast_in_dim.36), channel_id=1, replica_groups=mesh['slab_0'=8,'slab_1'=4,'slab_2'=8,'slab_3'=2] {'slab_1','slab_2','sl..., dimensions={0} | all-to-all | bytes 393216 | tf_op jit(solution)/shard_map/all_to_all | solution.py:29
  44.3 0.1 reduce_sum.48
  44.5 15.9 %all_to_all.13 = f32[8,1,768]{2,1,0:T(1,128)S(1)} all-to-all(f32[8,1,768]{2,1,0:T(1,128)S(1)} %broadcast_in_dim.66), channel_id=1, replica_groups=mesh['slab_0'=8,'slab_1'=4,'slab_2'=8,'slab_3'=2] {'slab_0'}, dimensions={0} | all-to-all | bytes 49152 | tf_op jit(solution)/shard_map/all_to_all | solution.py:29
  60.4 0.1 reshape.183
  60.5 0.0 copy-start.5
  60.5 0.1 reshape.184
  60.5 0.1 reshape.182
  60.6 0.1 copy.62
  60.7 0.1 fusion.57
  60.8 0.2 fusion.1
  61.0 0.2 convolution_add_fusion
  61.2 0.1 copy.64
  61.3 1.5 %cholesky.16 = f32[16,16]{1,0:T(8,128)S(1)} custom-call(f32[16,16]{1,0:T(8,128)S(1)} %fusion.53), custom_call_target="Cholesky" | custom-call | tf_op jit(solution)/shard_map/jit(cholesky)/cholesky | solution.py:130
  62.8 0.6 compare_reduce_fusion
  63.5 0.6 fusion.54
  64.1 1.2 %custom-call.6 = f32[1,16,16]{1,2,0:T(8,128)S(1)} custom-call(f32[1,16,16]{2,1,0:T(8,128)S(1)} %get-tuple-element.61), custom_call_target="InvertDiagBlocksLowerTriangular" | custom-call | tf_op jit(solution)/shard_map/triangular_solve | solution.py:134
  65.3 2.0 %fusion = f32[2,8,128,128]{3,1,2,0:T(8,128)S(1)} fusion(f32[16,16]{1,0:T(8,128)S(1)} %reshape.183, f32[2,8,128,128]{3,2,1,0:T(8,128)S(1)} %bitcast.75, f32[2,8,128,128]{3,2,1,0:T(8,128)S(1)} %bitcast.76), kind=kOutput, calls=%fused_computation.5 | convolution fusion | flops 50593792 | bytes 3146752 | tf_op jit(solution)/shard_map/dot_general | solution.py:131
  67.4 0.0 copy-done.5
  67.4 0.2 copy.83
  67.6 1.5 %fusion.20 = f32[16,8,16,128]{3,0,2,1:T(8,128)S(1)} fusion(f32[8,16,128,16]{2,1,0,3:T(8,128)S(1)} %bitcast.77, f32[1,16,16]{1,2,0:T(8,128)S(1)} %custom-call.6), kind=kOutput, calls=%fused_computation.30 | convolution fusion | flops 50331648 | bytes 2098176 | tf_op jit(solution)/shard_map/triangular_solve | solution.py:134
  69.1 1.3 %copy.67 = f32[16,8,16,128]{3,2,1,0:T(8,128)} copy(f32[16,8,16,128]{3,0,2,1:T(8,128)S(1)} %fusion.20) | data formatting | bytes 2097152
  70.4 0.7 copy.68
  (11 shorter events, 0.2 us)
Async XLA Ops:
  0.6 12.2 %copy-start = (f32[16,8,16,128]{3,2,1,0:T(8,128)S(1)}, f32[16,8,16,128]{3,2,1,0:T(8,128)}, u32[]{:S(2)}) copy-start(f32[16,8,16,128]{3,2,1,0:T(8,128)} %param.10) | copy-start | bytes 3145732
  2.8 12.2 %collective-permute-start = (f32[17,1,16,128]{3,2,1,0:T(8,128)S(1)}, f32[17,1,16,128]{3,2,1,0:T(8,128)S(1)}, u32[]{:S(2)}, u32[]{:S(2)}) collective-permute-start(f32[17,1,16,128]{3,2,1,0:T(8,128)S(1)} %get-tuple-element.43), channel_id=1, source_target_pairs={{0,1},{1,2},{2,3},{3,4},{4,5},{5,6},{6,7},{7,8},{8,9},{9,10},{10,1... | collective-permute-start | bytes 417800 | tf_op jit(solution)/shard_map/ppermute | solution.py:18
  7.4 7.6 %collective-permute-start.1 = (f32[17,1,16,128]{3,2,1,0:T(8,128)S(1)}, f32[17,1,16,128]{3,2,1,0:T(8,128)S(1)}, u32[]{:S(2)}, u32[]{:S(2)}) collective-permute-start(f32[17,1,16,128]{3,2,1,0:T(8,128)S(1)} %get-tuple-element.42), channel_id=1, source_target_pairs={{1,0},{2,1},{3,2},{4,3},{5,4},{6,5},{7,6},{8,7},{9,8},{10,9},{11,1... | collective-permute-start | bytes 417800 | tf_op jit(solution)/shard_map/ppermute | solution.py:20
  15.0 0.7 copy-start.3
  15.0 0.7 copy-start.1
  15.9 2.3 %copy-start.4 = (f32[17,1,16,128]{3,2,1,0:T(8,128)S(1)}, f32[17,1,16,128]{3,2,1,0:T(8,128)}, u32[]{:S(2)}) copy-start(f32[17,1,16,128]{3,2,1,0:T(8,128)} %copy-done.3) | copy-start | bytes 417796
  16.0 2.3 %copy-start.2 = (f32[17,1,16,128]{3,2,1,0:T(8,128)S(1)}, f32[17,1,16,128]{3,2,1,0:T(8,128)}, u32[]{:S(2)}) copy-start(f32[17,1,16,128]{3,2,1,0:T(8,128)} %copy-done.1) | copy-start | bytes 417796
  60.5 6.9 %copy-start.5 = (f32[16,16]{1,0:T(8,128)}, f32[16,16]{1,0:T(8,128)S(1)}, u32[]{:S(2)}) copy-start(f32[16,16]{1,0:T(8,128)S(1)} %reshape.183) | copy-start | bytes 3076
where the time goes:
time: 71.5 us; the launch traced here: 71 us
  blocking collectives  37.1 us (52%)
  matrix products  10.2 us (14%)
  starting transfers between devices  10 us (14%)
  other arithmetic  8.94 us (13%)
  local copies, waits for them, and re-layouts  3.87 us (5%)
  between operations  0.88 us (1%)
    all_to_all x2, blocking collectives, sent_to_all(): lax.all_to_all(jnp.broadcast_to(x[None], (peers, *x.shape)), axis, 0, 0,...  37.1 us
    dot_general x4, matrix products, block_products(): return jnp.dot(left, right.T, precision=lax.Precision.HIGHEST)  6.36 us
    ppermute x1, starting transfers between devices, extended(): lax.ppermute(head, axis, [((i + 1) % count, i) for i in range(ends)])  5.46 us
    ppermute x1, starting transfers between devices, extended(): lax.ppermute(tail, axis, [(i, (i + 1) % count) for i in range(ends)])  4.58 us
    unnamed x15, local copies, waits for them, and re-layouts  2.79 us
    add x1, other arithmetic, operate(): total = total + bond * (center_coefficient - neighbour_coefficient)  2.22 us
    another operation x3, other arithmetic, shards(): lower = jnp.linalg.cholesky(gram)  2.14 us
    dot_general x1, matrix products, shards(): jnp.dot(projection.T, basis_matrix, precision=lax.Precision.HIGHEST)  2 us
  transfers between devices with their start and end apart: 2, of which 0 were waited for; matrix products, arithmetic and copies ran while one was open for 3% of the time, Pallas kernels for 0%

commit v1 on v0

v1 whole, which is shorter than its diff:
```python
import functools

import jax
import jax.numpy as jnp
from jax import lax
from jax.experimental import pallas as pl
from jax.experimental.pallas import tpu as pltpu
from jax.sharding import Mesh
from jax.sharding import PartitionSpec as P

SLAB = ("slab_0", "slab_1", "slab_2", "slab_3")
NV, NX, NY, NZ, NR = 16, 8, 16, 128, 8
CELLS = 4096 * 16 * 128
F32, BF16 = jnp.float32, jnp.bfloat16
SMEM = pl.BlockSpec(memory_space=pltpu.SMEM)
VMEM = pl.BlockSpec(memory_space=pltpu.VMEM)


def table_at(region, table):
    out = jnp.zeros(region.shape, F32)
    for r in range(NR):
        out = jnp.where(region == r, table[r], out)
    return out


def two_parts(x):
    high = x.astype(BF16)
    return high, (x - high.astype(F32)).astype(BF16)


def pack_kernel(core, dens, v_ref, region_ref, out_ref):
    out_ref[0:NV] = v_ref[:, 0]
    out_ref[NV] = table_at(region_ref[0], dens)


def pack(core, side, dens, basis, region):
    def plane(core_ref):
        return (NX - 1) * (1 - core_ref[0]) if side == 0 else (NX - 1) * core_ref[0]

    return pl.pallas_call(
        pack_kernel,
        out_shape=jax.ShapeDtypeStruct((NV + 1, NY, NZ), F32),
        grid_spec=pltpu.PrefetchScalarGridSpec(
            num_scalar_prefetch=1,
            grid=(1,),
            in_specs=[
                SMEM,
                pl.BlockSpec((NV, 1, NY, NZ), lambda g, c: (0, plane(c), 0, 0)),
                pl.BlockSpec((1, NY, NZ), lambda g, c: (plane(c), 0, 0)),
            ],
            out_specs=pl.BlockSpec((NV + 1, NY, NZ), lambda g, c: (0, 0, 0)),
        ),
        compiler_params=pltpu.CompilerParams(vmem_limit_bytes=4 << 20),
        cost_estimate=pl.CostEstimate(flops=1 << 16, bytes_accessed=1 << 18, transcendentals=0),
        name="pack" + str(side),
    )(core, dens, basis, region)


def folded(full):
    rows = lax.broadcasted_iota(jnp.int32, (256, 256), 0)
    cols = lax.broadcasted_iota(jnp.int32, (256, 256), 1)
    kept = jnp.where(rows % 8 == cols % 8, full, 0.0)
    by_row = jnp.sum(kept.reshape(32, 8, 256), axis=1)
    pick = lax.broadcasted_iota(jnp.int32, (256, 128), 0) // 8
    lane = lax.broadcasted_iota(jnp.int32, (256, 128), 1)
    return jnp.dot(by_row, jnp.where(pick == lane, 1.0, 0.0).astype(F32), precision=lax.Precision.HIGHEST)


def products(high, low):
    dims = (((1,), (1,)), ((), ()))
    hh = lax.dot_general(high, high, dims, preferred_element_type=F32)
    hl = lax.dot_general(high, low, dims, preferred_element_type=F32)
    return hh, hl


def main_kernel(dens, stiff, dampt, v_ref, comp_ref, region_ref, x_ref, edge_ref, hh_ref, hl_ref, cx_ref):
    for x in range(NX):
        cx_ref[x] = table_at(region_ref[x], dens)
    yi = lax.broadcasted_iota(jnp.int32, (NY, NZ), 0)
    zi = lax.broadcasted_iota(jnp.int32, (NY, NZ), 1)
    for x in range(NX):
        c = cx_ref[x]
        diag = -table_at(region_ref[x], stiff)
        damp = table_at(region_ref[x], dampt)
        xs = []
        for xn in (x - 1, x + 1):
            if 0 <= xn < NX:
                b = 0.5 * (c + cx_ref[xn])
                diag = diag + b
                xs.append((xn, b))
        sides = []
        for shift, axis, end, at in ((NY - 1, 0, NY - 1, yi), (1, 0, 0, yi), (NZ - 1, 1, NZ - 1, zi), (1, 1, 0, zi)):
            outside = at == end
            b = jnp.where(outside, c, 0.5 * (c + pltpu.roll(c, shift, axis)))
            diag = diag + b
            sides.append((shift, axis, jnp.where(outside, 0.0, b)))

        def one(i, x=x, diag=diag, damp=damp, xs=xs, sides=sides):
            v = v_ref[i, x]
            f = diag * v + damp * comp_ref[i, x]
            for xn, b in xs:
                f = f - b * v_ref[i, xn]
            for shift, axis, b in sides:
                f = f - b * pltpu.roll(v, shift, axis)
            return v, f

        if 0 < x < NX - 1:

            def pair(p, carry, x=x, one=one):
                (v0, f0), (v1, f1) = one(2 * p), one(2 * p + 1)
                rows = pl.multiple_of(16 * p, 16)
                for h in range(2):
                    cols = pl.ds(((x - 1) * 2 + h) * NZ, NZ)
                    s = slice(8 * h, 8 * h + 8)
                    fh, fl = two_parts(jnp.concatenate([f0[s], f1[s]], axis=0))
                    vh, vl = two_parts(jnp.concatenate([v0[s], v1[s]], axis=0))
                    x_ref[pl.ds(rows, 16), cols] = fh
                    x_ref[pl.ds(rows + 128, 16), cols] = vh
                    x_ref[pl.ds(rows + 256, 16), cols] = fl
                    x_ref[pl.ds(rows + 384, 16), cols] = vl
                return carry

            lax.fori_loop(0, NV // 2, pair, 0, unroll=4)
        else:
            e = 0 if x == 0 else 1

            def single(i, carry, e=e, one=one):
                edge_ref[e, i] = one(i)[1]
                return carry

            lax.fori_loop(0, NV, single, 0, unroll=4)
    hh, hl = products(x_ref[0:256], x_ref[256:512])
    hh_ref[...] = hh
    hl_ref[...] = hl


def main(dens, stiff, dampt, basis, companion, region):
    return pl.pallas_call(
        main_kernel,
        out_shape=(
            jax.ShapeDtypeStruct((512, 1536), BF16),
            jax.ShapeDtypeStruct((2, NV, NY, NZ), F32),
            jax.ShapeDtypeStruct((256, 256), F32),
            jax.ShapeDtypeStruct((256, 256), F32),
        ),
        in_specs=[SMEM] * 3 + [VMEM] * 3,
        out_specs=(VMEM,) * 4,
        scratch_shapes=[pltpu.VMEM((NX, NY, NZ), F32)],
        compiler_params=pltpu.CompilerParams(vmem_limit_bytes=16 << 20),
        cost_estimate=pl.CostEstimate(flops=1 << 28, bytes_accessed=5 << 20, transcendentals=0),
        name="main",
    )(dens, stiff, dampt, basis, companion, region)


def edge_kernel(core, edge_ref, hh_ref, hl_ref, own0, own1, got0, got1, x_ref, out_ref):
    upper = (1 - core[0], core[0])
    for side, (own, got) in enumerate(((own0, got0), (own1, got1))):
        place = upper[side]
        c, other = own[NV], got[NV]
        b = 0.5 * (c + jnp.where(other > 0.0, other, c))

        def pair(p, carry, own=own, got=got, place=place, b=b):
            fs, vs = [], []
            for i in (2 * p, 2 * p + 1):
                v = own[i]
                fs.append(edge_ref[place, i] + b * (v - got[i]))
                vs.append(v)
            rows = pl.multiple_of(16 * p, 16)
            for h in range(2):
                cols = pl.ds(pl.multiple_of((place * 2 + h) * NZ, NZ), NZ)
                s = slice(8 * h, 8 * h + 8)
                fh, fl = two_parts(jnp.concatenate([fs[0][s], fs[1][s]], axis=0))
                vh, vl = two_parts(jnp.concatenate([vs[0][s], vs[1][s]], axis=0))
                x_ref[pl.ds(rows, 16), cols] = fh
                x_ref[pl.ds(rows + 128, 16), cols] = vh
                x_ref[pl.ds(rows + 256, 16), cols] = fl
                x_ref[pl.ds(rows + 384, 16), cols] = vl
            return carry

        lax.fori_loop(0, NV // 2, pair, 0, unroll=4)
    hh, hl = products(x_ref[0:256], x_ref[256:512])
    same = folded(hh + hh_ref[...])
    mixed = folded(hl + hl_ref[...])
    eye = jnp.where(
        lax.broadcasted_iota(jnp.int32, (32, 128), 0) == lax.broadcasted_iota(jnp.int32, (32, 128), 1), 1.0, 0.0
    ).astype(F32)
    turned = lax.dot_general(eye, mixed, (((1,), (1,)), ((), ())), precision=lax.Precision.HIGHEST)
    turned = jnp.pad(turned, ((0, 0), (0, 96)))
    total = (same + mixed + turned) * (1.0 / CELLS)
    lanes = total[16:32] + pltpu.roll(total[0:16], 32, 1)
    out_ref[...] = lanes[0:8] + pltpu.roll(lanes[8:16], 64, 1)


def edge(core, edges, hh, hl, own, got):
    return pl.pallas_call(
        edge_kernel,
        out_shape=(jax.ShapeDtypeStruct((512, 512), BF16), jax.ShapeDtypeStruct((8, 128), F32)),
        in_specs=[SMEM] + [VMEM] * 7,
        out_specs=(VMEM, VMEM),
        compiler_params=pltpu.CompilerParams(vmem_limit_bytes=8 << 20),
        cost_estimate=pl.CostEstimate(flops=1 << 27, bytes_accessed=2 << 20, transcendentals=0),
        name="edge",
    )(core, edges, hh, hl, *own, *got)


def finish_kernel(parts_ref, xi_ref, xe_ref, new_ref, proj_ref, r_ref, stage, sems):
    packed = jnp.sum(parts_ref[...], axis=0)
    lanes = jnp.concatenate([packed, pltpu.roll(packed, 64, 1)], axis=0)
    vf, vv, ff, fv = (lanes[:, 16 * k : 16 * k + 16] for k in range(4))
    proj_ref[...] = vf
    exact = functools.partial(jnp.dot, precision=lax.Precision.HIGHEST, preferred_element_type=F32)
    gram = ff + exact(fv, exact(vv, vf) - 2.0 * vf)
    row = lax.broadcasted_iota(jnp.int32, (NV, 128), 0)
    lane = lax.broadcasted_iota(jnp.int32, (NV, 128), 1)
    unit = jnp.where(row + 16 == lane, 1.0, 0.0).astype(F32)
    shifted_fv = jnp.where((lane >= 32) & (lane < 48), pltpu.roll(lanes, 128 - 16, 1), 0.0)
    a = jnp.pad(gram, ((0, 0), (0, 112))) + unit + shifted_fv
    for k in range(NV - 1):
        col = jnp.broadcast_to(a[:, k : k + 1], (NV, 128))
        pivot = jnp.broadcast_to(col[k : k + 1], (NV, 128))
        factor = jnp.where(row > k, col / pivot, 0.0)
        a = a - factor * jnp.broadcast_to(a[k : k + 1], (NV, 128))
    pivots = jnp.sum(jnp.where(row == lane, a, 0.0), axis=1, keepdims=True)
    a = a / jnp.sqrt(pivots)
    r_ref[...] = jnp.where(lane >= row, a, 0.0)[:, 0:NV]
    w = jnp.where(lane < 32, a, -a)
    w = jnp.broadcast_to(w[:, None, :], (NV, 8, 128)).reshape(128, 128)
    wh, wl = two_parts(w)
    source = lax.broadcasted_iota(jnp.int32, (128, 256), 0)
    target = lax.broadcasted_iota(jnp.int32, (128, 256), 1)
    spread = jnp.where(source - 16 == target // 8, 1.0, 0.0).astype(BF16)
    keep = source % 8 == target % 8
    kh, kl = (
        jnp.where(keep, jnp.dot(part, spread, preferred_element_type=F32), 0.0).astype(BF16) for part in (wh, wl)
    )
    khh = jnp.concatenate([kh, kh], axis=1)

    def planes(x_ref, at):
        cols = slice(256 * at, 256 * at + 256)
        return jnp.dot(khh, x_ref[:, cols], preferred_element_type=F32) + jnp.dot(
            kl, x_ref[0:256, cols], preferred_element_type=F32
        )

    copies = []
    for x in range(NX):
        got = planes(xe_ref, 0 if x == 0 else 1) if x in (0, NX - 1) else planes(xi_ref, x - 1)
        for h in range(2):
            stage[:, x, 8 * h : 8 * h + 8, :] = got[:, NZ * h : NZ * h + NZ].reshape(NV, 8, NZ)
        if x % 2:
            pair = pl.ds(x - 1, 2)
            copy = pltpu.make_async_copy(stage.at[:, pair], new_ref.at[:, pair], sems.at[x // 2])
            copy.start()
            copies.append(copy)
    for copy in copies:
        copy.wait()


def finish(parts, xi, xe):
    return pl.pallas_call(
        finish_kernel,
        out_shape=(
            jax.ShapeDtypeStruct((NV, NX, NY, NZ), F32),
            jax.ShapeDtypeStruct((NV, NV), F32),
            jax.ShapeDtypeStruct((NV, NV), F32),
        ),
        in_specs=[VMEM] * 3,
        out_specs=(pl.BlockSpec(memory_space=pl.ANY), VMEM, VMEM),
        scratch_shapes=[pltpu.VMEM((NV, NX, NY, NZ), F32), pltpu.SemaphoreType.DMA((NX // 2,))],
        compiler_params=pltpu.CompilerParams(vmem_limit_bytes=16 << 20),
        cost_estimate=pl.CostEstimate(flops=1 << 29, bytes_accessed=3 << 20, transcendentals=0),
        name="finish",
    )(parts, xi, xe)


def sent_to_all(x, axes):
    peers = lax.axis_size(axes)
    return lax.all_to_all(jnp.broadcast_to(x[None], (peers, *x.shape)), axes, 0, 0, tiled=True)


def shards(krylov_basis_block, companion, region, inv_density, stiffness, damping):
    core = lax.axis_index("slab_3").astype(jnp.int32).reshape(1)
    count = lax.axis_size(SLAB)
    own = [pack(core, side, inv_density, krylov_basis_block, region) for side in (0, 1)]
    pairs = [(i, i ^ 1) for i in range(count)]
    across = [(i, i + 1 if i % 2 else i - 1) for i in range(1, count - 1)]
    got1 = lax.ppermute(own[1], SLAB, across)
    got0 = lax.ppermute(own[0], SLAB, pairs)
    xi, edges, hh, hl = main(inv_density, stiffness, damping, krylov_basis_block, companion, region)
    xe, packed = edge(core, edges, hh, hl, own, (got0, got1))
    near = sent_to_all(packed.reshape(1, 1024), ("slab_1", "slab_2")).sum(axis=0)
    far = sent_to_all(near.reshape(1, 1024), ("slab_0", "slab_3"))
    new_block, projection, rfactor = finish(far.reshape(-1, 8, 128), xi, xe)
    return new_block, projection, rfactor


def solution(mesh):
    torus = Mesh(mesh.devices.reshape(8, 4, 8, 2), SLAB)
    placed = (
        P(None, SLAB, None, None),
        P(None, SLAB, None, None),
        P(SLAB, None, None),
        P(),
        P(),
        P(),
    )
    return jax.shard_map(
        shards,
        mesh=torus,
        in_specs=placed,
        out_specs=(P(None, SLAB, None, None), P(), P()),
        check_vma=False,
    )
```

time: 71.5 us -> 60.4 us (0.84)
  Pallas kernels: 0 us -> 10.3 us
  matrix products: 10.2 us -> 0 us
  other arithmetic: 8.94 us -> 0.09 us
  blocking collectives: 37.1 us -> 34.5 us
  local copies, waits for them, and re-layouts: 3.87 us -> 2.86 us
  starting transfers between devices: 10 us -> 10.8 us
    pallas_call x0 -> x5, Pallas kernels: none -> 10.3 us  [the longest x1 4.36 us: finish(): pl.pallas_call(finish_kernel, out_shape=(jax.ShapeDtypeStruct((NV, NX, NY...]
    dot_general x7 -> x0, matrix products: 8.7 us -> none  [the longest x4 6.36 us: block_products(): return jnp.dot(left, right.T, precision=lax.Precision.HIGHEST)]
    another operation x4 -> x0, other arithmetic: 3.37 us -> none  [the longest x3 2.14 us: shards(): lower = jnp.linalg.cholesky(gram)]
    all_to_all x2, blocking collectives: 37.1 us -> 34.5 us  [sent_to_all(): lax.all_to_all(jnp.broadcast_to(x[None], (peers, *x.shape)), axes, 0, 0,...]
    add x1 -> x0, other arithmetic: 2.22 us -> none  [operate(): total = total + bond * (center_coefficient - neighbour_coefficient)]
    another operation x1 -> x0, matrix products: 1.5 us -> none  [shards(): lax.linalg.triangular_solve(lower, reduced_products, left_side=True, lowe...]
    reduce_sum x3 -> x1, other arithmetic: 1.33 us -> 0.09 us  [shards(): sent_to_all(packed.reshape(1, 1024), ('slab_1', 'slab_2')).sum(axis=0)]
    concatenate x4 -> x0, other arithmetic: 1.04 us -> none  [the longest x1 1 us: shards(): stacked = jnp.concatenate([krylov_basis_block, coef[None]], axis=0)]
  transfers between devices with their start and end apart: 2 -> 2, of which waited for: 0 -> 1; matrix products, arithmetic and copies ran while one was open for 3% -> 0% of each run, Pallas kernels for 0% -> 7%
where the time goes in v1:
time: 60.4 us; the launch traced here: 60.1 us
  blocking collectives  34.5 us (57%)
  starting transfers between devices  10.8 us (18%)
  Pallas kernels  10.3 us (17%)
  local copies, waits for them, and re-layouts  2.86 us (5%)
  between operations  0.78 us (1%)
  waiting for transfers between devices  0.7 us (1%)
    all_to_all x2, blocking collectives, sent_to_all(): lax.all_to_all(jnp.broadcast_to(x[None], (peers, *x.shape)), axes, 0, 0,...  34.5 us
    ppermute x1, starting transfers between devices, shards(): got0 = lax.ppermute(own[0], SLAB, pairs)  8.88 us
    pallas_call x1, Pallas kernels, finish(): pl.pallas_call(finish_kernel, out_shape=(jax.ShapeDtypeStruct((NV, NX, NY...  4.36 us
    pallas_call x1, Pallas kernels, main(): pl.pallas_call(main_kernel, out_shape=(jax.ShapeDtypeStruct((512, 1536),...  3.67 us
    unnamed x18, local copies, waits for them, and re-layouts  2.75 us
    ppermute x1, starting transfers between devices, shards(): got1 = lax.ppermute(own[1], SLAB, across)  1.92 us
  transfers between devices with their start and end apart: 2, of which 1 were waited for; matrix products, arithmetic and copies ran while one was open for 0% of the time, Pallas kernels for 7%

profile of v1, /device:TPU:1, one launch (start us, length us, event | category | flops | bytes accessed | tf_op | source)
XLA Modules:
  0.0 60.1 jit_solution(5866082466548707402)
XLA Ops:
  0.6 0.0 copy-start.6
  0.6 0.0 copy-start.8
  0.7 0.0 copy-start.7
  0.7 0.0 copy-start
  0.7 1.2 %copy-done = f32[16,8,16,128]{3,2,1,0:T(8,128)S(1)} copy-done((f32[16,8,16,128]{3,2,1,0:T(8,128)S(1)}, f32[16,8,16,128]{3,2,1,0:T(8,128)}, u32[]{:S(2)}) %copy-start) | copy-done | bytes 1048600
  1.9 0.0 copy-start.3
  1.9 0.8 %copy-done.3 = s32[8,16,128]{2,1,0:T(8,128)S(1)} copy-done((s32[8,16,128]{2,1,0:T(8,128)S(1)}, s32[8,16,128]{2,1,0:T(8,128)}, u32[]{:S(2)}) %copy-start.3) | copy-done | bytes 65560
  2.7 0.0 copy-start.5
  2.7 0.7 %copy-done.5 = f32[8]{0:T(128)S(1)} copy-done((f32[8]{0:T(128)S(1)}, f32[8]{0:T(128)}, u32[]{:S(2)}) %copy-start.5) | copy-done | bytes 56
  3.4 0.0 copy-start.1
  3.4 0.0 copy-start.2
  3.4 0.0 copy-start.4
  3.4 0.6 pack0.1.own0
  4.0 8.9 %collective-permute-start = (f32[17,16,128]{2,1,0:T(8,128)S(1)}, f32[17,16,128]{2,1,0:T(8,128)S(1)}, u32[]{:S(2)}, u32[]{:S(2)}) collective-permute-start(f32[17,16,128]{2,1,0:T(8,128)S(1)} %pack0.1.own0), channel_id=1, source_target_pairs={{0,1},{1,0},{2,3},{3,2},{4,5},{5,4},{6,7},{7,6},{8,9},{9,8},{10,11... | collective-permute-start | bytes 417800 | tf_op jit(solution)/shard_map/ppermute | solution.py:287
  12.9 0.6 pack1.1.own1
  13.4 1.9 %collective-permute-start.1 = (f32[17,16,128]{2,1,0:T(8,128)S(1)}, f32[17,16,128]{2,1,0:T(8,128)S(1)}, u32[]{:S(2)}, u32[]{:S(2)}) collective-permute-start(f32[17,16,128]{2,1,0:T(8,128)S(1)} %pack1.1.own1), channel_id=1, source_target_pairs={{1,2},{2,1},{3,4},{4,3},{5,6},{6,5},{7,8},{8,7},{9,10},{10,9},{11,... | collective-permute-start | bytes 417800 | tf_op jit(solution)/shard_map/ppermute | solution.py:286
  15.3 0.0 copy-done.6
  15.4 0.0 copy-done.8
  15.4 0.0 copy-done.7
  15.4 0.0 copy-done.1
  15.4 0.0 copy-done.2
  15.4 0.0 copy-done.4
  15.4 3.7 %main.1 = (bf16[512,1536]{1,0:T(8,128)(2,1)S(1)}, f32[2,16,16,128]{3,2,1,0:T(8,128)S(1)}, f32[256,256]{1,0:T(8,128)S(1)}, f32[256,256]{1,0:T(8,128)S(1)}) custom-call(f32[8]{0:T(128)S(1)} %copy-done.6, f32[8]{0:T(128)S(1)} %copy-done.7, f32[8]{0:T(128)S(1)} %copy-done.8, f32[16,8,16,128]{3,2,1,0:T(8,128)S(1)} %copy-done.1, f32[16,8,16,128]{3,2,1,0:T(8,128)S(1)} %copy-done.2, ...), custom_call_target="tpu_custom_call" | custom-call | flops 268435456 | bytes 5242880 | tf_op jit(solution)/shard_map/main/pallas_call | solution.py:138
  19.1 0.0 collective-permute-done.got0
  19.1 0.7 %collective-permute-done.1.got1 = f32[17,16,128]{2,1,0:T(8,128)S(1)} collective-permute-done((f32[17,16,128]{2,1,0:T(8,128)S(1)}, f32[17,16,128]{2,1,0:T(8,128)S(1)}, u32[]{:S(2)}, u32[]{:S(2)}) %collective-permute-start.1) | collective-permute-done | bytes 139296 | tf_op jit(solution)/shard_map/ppermute | solution.py:286
  19.8 1.2 %edge.1 = (bf16[512,512]{1,0:T(8,128)(2,1)S(1)}, f32[8,128]{1,0:T(8,128)S(1)}) custom-call(s32[1]{0:T(128)} %bitcast.core, f32[2,16,16,128]{3,2,1,0:T(8,128)S(1)} %get-tuple-element.9.edge_ref, f32[256,256]{1,0:T(8,128)S(1)} %get-tuple-element.10.hh_ref, f32[256,256]{1,0:T(8,128)S(1)} %get-tuple-element.11.hl_ref, f32[17,16,128]{2,1,0:T(8,128)S(1)} %pack0.1.own0, ...), custom_call_target="tpu_custom_call" | custom-call | flops 134217728 | bytes 2097152 | tf_op jit(solution)/shard_map/edge/pallas_call | solution.py:195
  20.9 0.1 broadcast_in_dim.14
  21.0 15.2 %all_to_all.10 = f32[32,1,1024]{2,1,0:T(1,128)S(1)} all-to-all(f32[32,1,1024]{2,1,0:T(1,128)S(1)} %broadcast_in_dim.14), channel_id=1, replica_groups=mesh['slab_0'=8,'slab_1'=4,'slab_2'=8,'slab_3'=2] {'slab_1','slab_2'}, dimensions={0} | all-to-all | bytes 262144 | tf_op jit(solution)/shard_map/all_to_all | solution.py:277
  36.2 0.1 reduce_sum.9
  36.3 19.4 %all_to_all.11 = f32[16,1,1024]{2,1,0:T(1,128)S(1)} all-to-all(f32[16,1,1024]{2,1,0:T(1,128)S(1)} %broadcast_in_dim.15), channel_id=1, replica_groups=mesh['slab_0'=8,'slab_1'=4,'slab_2'=8,'slab_3'=2] {'slab_0','slab_3'}, dimensions={0} | all-to-all | bytes 131072 | tf_op jit(solution)/shard_map/all_to_all | solution.py:277
  55.7 4.4 %finish.1 = (f32[16,8,16,128]{3,2,1,0:T(8,128)}, f32[16,16]{1,0:T(8,128)}, f32[16,16]{1,0:T(8,128)}) custom-call(f32[16,8,128]{2,1,0:T(8,128)S(1)} %bitcast.3, bf16[512,1536]{1,0:T(8,128)(2,1)S(1)} %get-tuple-element.13.xi_ref, bf16[512,512]{1,0:T(8,128)(2,1)S(1)} %get-tuple-element.14.xe_ref), custom_call_target="tpu_custom_call" | custom-call | flops 536870912 | bytes 3145728 | tf_op jit(solution)/shard_map/finish/pallas_call | solution.py:259
  (1 shorter events, 0.0 us)
Async XLA Ops:
  0.6 14.7 %copy-start.6 = (f32[8]{0:T(128)S(1)}, f32[8]{0:T(128)}, u32[]{:S(2)}) copy-start(f32[8]{0:T(128)} %dens.5) | copy-start | bytes 100
  0.6 14.7 %copy-start.8 = (f32[8]{0:T(128)S(1)}, f32[8]{0:T(128)}, u32[]{:S(2)}) copy-start(f32[8]{0:T(128)} %dampt.1) | copy-start | bytes 100
  0.7 14.7 %copy-start.7 = (f32[8]{0:T(128)S(1)}, f32[8]{0:T(128)}, u32[]{:S(2)}) copy-start(f32[8]{0:T(128)} %stiff.1) | copy-start | bytes 100
  0.7 1.2 %copy-start = (f32[16,8,16,128]{3,2,1,0:T(8,128)S(1)}, f32[16,8,16,128]{3,2,1,0:T(8,128)}, u32[]{:S(2)}) copy-start(f32[16,8,16,128]{3,2,1,0:T(8,128)} %v_ref.5) | copy-start | bytes 3145732
  1.9 0.8 %copy-start.3 = (s32[8,16,128]{2,1,0:T(8,128)S(1)}, s32[8,16,128]{2,1,0:T(8,128)}, u32[]{:S(2)}) copy-start(s32[8,16,128]{2,1,0:T(8,128)} %region_ref.5) | copy-start | bytes 196612
  2.7 0.7 %copy-start.5 = (f32[8]{0:T(128)S(1)}, f32[8]{0:T(128)}, u32[]{:S(2)}) copy-start(f32[8]{0:T(128)} %dens.5) | copy-start | bytes 100
  3.4 12.0 %copy-start.1 = (f32[16,8,16,128]{3,2,1,0:T(8,128)S(1)}, f32[16,8,16,128]{3,2,1,0:T(8,128)}, u32[]{:S(2)}) copy-start(f32[16,8,16,128]{3,2,1,0:T(8,128)} %v_ref.5) | copy-start | bytes 3145732
  3.4 12.0 %copy-start.2 = (f32[16,8,16,128]{3,2,1,0:T(8,128)S(1)}, f32[16,8,16,128]{3,2,1,0:T(8,128)}, u32[]{:S(2)}) copy-start(f32[16,8,16,128]{3,2,1,0:T(8,128)} %comp_ref.1) | copy-start | bytes 3145732
  3.4 12.0 %copy-start.4 = (s32[8,16,128]{2,1,0:T(8,128)S(1)}, s32[8,16,128]{2,1,0:T(8,128)}, u32[]{:S(2)}) copy-start(s32[8,16,128]{2,1,0:T(8,128)} %region_ref.5) | copy-start | bytes 196612
  4.0 15.1 %collective-permute-start = (f32[17,16,128]{2,1,0:T(8,128)S(1)}, f32[17,16,128]{2,1,0:T(8,128)S(1)}, u32[]{:S(2)}, u32[]{:S(2)}) collective-permute-start(f32[17,16,128]{2,1,0:T(8,128)S(1)} %pack0.1.own0), channel_id=1, source_target_pairs={{0,1},{1,0},{2,3},{3,2},{4,5},{5,4},{6,7},{7,6},{8,9},{9,8},{10,11... | collective-permute-start | bytes 417800 | tf_op jit(solution)/shard_map/ppermute | solution.py:287
  13.4 6.4 %collective-permute-start.1 = (f32[17,16,128]{2,1,0:T(8,128)S(1)}, f32[17,16,128]{2,1,0:T(8,128)S(1)}, u32[]{:S(2)}, u32[]{:S(2)}) collective-permute-start(f32[17,16,128]{2,1,0:T(8,128)S(1)} %pack1.1.own1), channel_id=1, source_target_pairs={{1,2},{2,1},{3,4},{4,3},{5,6},{6,5},{7,8},{8,7},{9,10},{10,9},{11,... | collective-permute-start | bytes 417800 | tf_op jit(solution)/shard_map/ppermute | solution.py:286

commit v2 on v1

--- a/solution.py
+++ b/solution.py
@@ -12,15 +12,9 @@
 NV, NX, NY, NZ, NR = 16, 8, 16, 128, 8
 CELLS = 4096 * 16 * 128
 F32, BF16 = jnp.float32, jnp.bfloat16
+UNROLL = 4
 SMEM = pl.BlockSpec(memory_space=pltpu.SMEM)
 VMEM = pl.BlockSpec(memory_space=pltpu.VMEM)
-
-
-def table_at(region, table):
-    out = jnp.zeros(region.shape, F32)
-    for r in range(NR):
-        out = jnp.where(region == r, table[r], out)
-    return out
 
 
 def two_parts(x):
@@ -28,32 +22,55 @@
     return high, (x - high.astype(F32)).astype(BF16)
 
 
-def pack_kernel(core, dens, v_ref, region_ref, out_ref):
-    out_ref[0:NV] = v_ref[:, 0]
-    out_ref[NV] = table_at(region_ref[0], dens)
-
-
-def pack(core, side, dens, basis, region):
-    def plane(core_ref):
-        return (NX - 1) * (1 - core_ref[0]) if side == 0 else (NX - 1) * core_ref[0]
-
+HBM = pl.BlockSpec(memory_space=pltpu.HBM)
+
+
+def in_hbm(*arrays):
+    return [pltpu.with_memory_space_constraint(a, pltpu.HBM) for a in arrays]
+
+
+def pack_kernel(core, dens_ref, stiff_ref, damp_ref, v_ref, region_ref, out0, out1, fields, tables, regions, sems):
+    outs = (out0, out1)
+    at = ((NX - 1) * core[0], (NX - 1) * (1 - core[0]))
+    whole = pltpu.make_async_copy(region_ref, regions, sems.at[0])
+    small = [
+        pltpu.make_async_copy(ref, tables.at[k], sems.at[1 + k]) for k, ref in enumerate((dens_ref, stiff_ref, damp_ref))
+    ]
+    planes = [pltpu.make_async_copy(v_ref.at[:, at[k]], outs[k].at[pl.ds(0, NV)], sems.at[4 + k]) for k in (0, 1)]
+    for copy in (whole, *small, *planes):
+        copy.start()
+    for copy in (*small, whole):
+        copy.wait()
+    for x in range(NX):
+        region = regions[x]
+        values = [jnp.zeros(region.shape, F32)] * 3
+        for r in range(NR):
+            here = region == r
+            values = [jnp.where(here, tables[k, r], values[k]) for k in range(3)]
+        for k in range(3):
+            fields[k, x] = values[k]
+    for k in (0, 1):
+        outs[k][NV] = fields[0, at[k]]
+    for copy in planes:
+        copy.wait()
+
+
+def pack(core, dens, stiff, dampt, basis, region):
+    plane = jax.ShapeDtypeStruct((NV + 1, NY, NZ), F32)
     return pl.pallas_call(
         pack_kernel,
-        out_shape=jax.ShapeDtypeStruct((NV + 1, NY, NZ), F32),
-        grid_spec=pltpu.PrefetchScalarGridSpec(
-            num_scalar_prefetch=1,
-            grid=(1,),
-            in_specs=[
-                SMEM,
-                pl.BlockSpec((NV, 1, NY, NZ), lambda g, c: (0, plane(c), 0, 0)),
-                pl.BlockSpec((1, NY, NZ), lambda g, c: (plane(c), 0, 0)),
-            ],
-            out_specs=pl.BlockSpec((NV + 1, NY, NZ), lambda g, c: (0, 0, 0)),
-        ),
+        out_shape=(plane, plane, jax.ShapeDtypeStruct((3, NX, NY, NZ), F32)),
+        in_specs=[SMEM] + [HBM] * 5,
+        out_specs=(VMEM,) * 3,
+        scratch_shapes=[
+            pltpu.SMEM((3, NR), F32),
+            pltpu.VMEM((NX, NY, NZ), jnp.int32),
+            pltpu.SemaphoreType.DMA((6,)),
+        ],
         compiler_params=pltpu.CompilerParams(vmem_limit_bytes=4 << 20),
-        cost_estimate=pl.CostEstimate(flops=1 << 16, bytes_accessed=1 << 18, transcendentals=0),
-        name="pack" + str(side),
-    )(core, dens, basis, region)
+        cost_estimate=pl.CostEstimate(flops=1 << 18, bytes_accessed=1 << 19, transcendentals=0),
+        name="pack",
+    )(core, *in_hbm(dens, stiff, dampt, basis, region))
 
 
 def folded(full):
@@ -73,19 +90,35 @@
     return hh, hl
 
 
-def main_kernel(dens, stiff, dampt, v_ref, comp_ref, region_ref, x_ref, edge_ref, hh_ref, hl_ref, cx_ref):
-    for x in range(NX):
-        cx_ref[x] = table_at(region_ref[x], dens)
+def main_kernel(v_ref, fields, comp_hbm, x_ref, edge_ref, hh_ref, hl_ref, comp_ref, sems):
+    order = (*range(1, NX - 1), 0, NX - 1)
+    copies = {x: pltpu.make_async_copy(comp_hbm.at[:, x], comp_ref.at[:, x], sems.at[x]) for x in order}
+    for x in order:
+        copies[x].start()
     yi = lax.broadcasted_iota(jnp.int32, (NY, NZ), 0)
     zi = lax.broadcasted_iota(jnp.int32, (NY, NZ), 1)
-    for x in range(NX):
-        c = cx_ref[x]
-        diag = -table_at(region_ref[x], stiff)
-        damp = table_at(region_ref[x], dampt)
+    for x in range(1, NX - 1):
+
+        def split(p, carry, x=x):
+            v0, v1 = v_ref[2 * p, x], v_ref[2 * p + 1, x]
+            rows = pl.multiple_of(16 * p, 16)
+            for h in range(2):
+                cols = pl.ds(((x - 1) * 2 + h) * NZ, NZ)
+                s = slice(8 * h, 8 * h + 8)
+                vh, vl = two_parts(jnp.concatenate([v0[s], v1[s]], axis=0))
+                x_ref[pl.ds(rows + 128, 16), cols] = vh
+                x_ref[pl.ds(rows + 384, 16), cols] = vl
+            return carry
+
+        lax.fori_loop(0, NV // 2, split, 0, unroll=UNROLL)
+    for x in order:
+        c = fields[0, x]
+        diag = -fields[1, x]
+        damp = fields[2, x]
         xs = []
         for xn in (x - 1, x + 1):
             if 0 <= xn < NX:
-                b = 0.5 * (c + cx_ref[xn])
+                b = 0.5 * (c + fields[0, xn])
                 diag = diag + b
                 xs.append((xn, b))
         sides = []
@@ -102,39 +135,37 @@
                 f = f - b * v_ref[i, xn]
             for shift, axis, b in sides:
                 f = f - b * pltpu.roll(v, shift, axis)
-            return v, f
-
+            return f
+
+        copies[x].wait()
         if 0 < x < NX - 1:
 
             def pair(p, carry, x=x, one=one):
-                (v0, f0), (v1, f1) = one(2 * p), one(2 * p + 1)
+                f0, f1 = one(2 * p), one(2 * p + 1)
                 rows = pl.multiple_of(16 * p, 16)
                 for h in range(2):
                     cols = pl.ds(((x - 1) * 2 + h) * NZ, NZ)
                     s = slice(8 * h, 8 * h + 8)
                     fh, fl = two_parts(jnp.concatenate([f0[s], f1[s]], axis=0))
-                    vh, vl = two_parts(jnp.concatenate([v0[s], v1[s]], axis=0))
                     x_ref[pl.ds(rows, 16), cols] = fh
-                    x_ref[pl.ds(rows + 128, 16), cols] = vh
                     x_ref[pl.ds(rows + 256, 16), cols] = fl
-                    x_ref[pl.ds(rows + 384, 16), cols] = vl
                 return carry
 
-            lax.fori_loop(0, NV // 2, pair, 0, unroll=4)
+            lax.fori_loop(0, NV // 2, pair, 0, unroll=UNROLL)
         else:
             e = 0 if x == 0 else 1
 
             def single(i, carry, e=e, one=one):
-                edge_ref[e, i] = one(i)[1]
+                edge_ref[e, i] = one(i)
                 return carry
 
-            lax.fori_loop(0, NV, single, 0, unroll=4)
+            lax.fori_loop(0, NV, single, 0, unroll=UNROLL)
     hh, hl = products(x_ref[0:256], x_ref[256:512])
     hh_ref[...] = hh
     hl_ref[...] = hl
 
 
-def main(dens, stiff, dampt, basis, companion, region):
+def main(basis, fields, companion):
     return pl.pallas_call(
         main_kernel,
         out_shape=(
@@ -143,17 +174,17 @@
             jax.ShapeDtypeStruct((256, 256), F32),
             jax.ShapeDtypeStruct((256, 256), F32),
         ),
-        in_specs=[SMEM] * 3 + [VMEM] * 3,
+        in_specs=[VMEM, VMEM, HBM],
         out_specs=(VMEM,) * 4,
-        scratch_shapes=[pltpu.VMEM((NX, NY, NZ), F32)],
+        scratch_shapes=[pltpu.VMEM((NV, NX, NY, NZ), F32), pltpu.SemaphoreType.DMA((NX,))],
         compiler_params=pltpu.CompilerParams(vmem_limit_bytes=16 << 20),
         cost_estimate=pl.CostEstimate(flops=1 << 28, bytes_accessed=5 << 20, transcendentals=0),
         name="main",
-    )(dens, stiff, dampt, basis, companion, region)
+    )(basis, fields, *in_hbm(companion))
 
 
 def edge_kernel(core, edge_ref, hh_ref, hl_ref, own0, own1, got0, got1, x_ref, out_ref):
-    upper = (1 - core[0], core[0])
+    upper = (core[0], 1 - core[0])
     for side, (own, got) in enumerate(((own0, got0), (own1, got1))):
         place = upper[side]
         c, other = own[NV], got[NV]
@@ -280,12 +311,12 @@
 def shards(krylov_basis_block, companion, region, inv_density, stiffness, damping):
     core = lax.axis_index("slab_3").astype(jnp.int32).reshape(1)
     count = lax.axis_size(SLAB)
-    own = [pack(core, side, inv_density, krylov_basis_block, region) for side in (0, 1)]
+    *own, fields = pack(core, inv_density, stiffness, damping, krylov_basis_block, region)
     pairs = [(i, i ^ 1) for i in range(count)]
     across = [(i, i + 1 if i % 2 else i - 1) for i in range(1, count - 1)]
-    got1 = lax.ppermute(own[1], SLAB, across)
-    got0 = lax.ppermute(own[0], SLAB, pairs)
-    xi, edges, hh, hl = main(inv_density, stiffness, damping, krylov_basis_block, companion, region)
+    got0 = lax.ppermute(own[0], SLAB, across)
+    got1 = lax.ppermute(own[1], SLAB, pairs)
+    xi, edges, hh, hl = main(krylov_basis_block, fields, companion)
     xe, packed = edge(core, edges, hh, hl, own, (got0, got1))
     near = sent_to_all(packed.reshape(1, 1024), ("slab_1", "slab_2")).sum(axis=0)
     far = sent_to_all(near.reshape(1, 1024), ("slab_0", "slab_3"))

time: 60.4 us -> 56.1 us (0.929)
  local copies, waits for them, and re-layouts: 2.86 us -> 0.11 us
  starting transfers between devices: 10.8 us -> 9.42 us
  waiting for transfers between devices: 0.7 us -> 0.01 us
    unnamed x18 -> x2, local copies, waits for them, and re-layouts: 2.75 us -> 0.01 us
    ppermute x2, starting transfers between devices: 10.8 us -> 9.42 us  [the longest x1 4.83 us: shards(): got1 = lax.ppermute(own[1], SLAB, pairs)]
    ppermute x2, waiting for transfers between devices: 0.7 us -> 0.01 us  [the longest x1 0.01 us: shards(): got1 = lax.ppermute(own[1], SLAB, pairs)]
  transfers between devices with their start and end apart: 2 -> 2, of which waited for: 1 -> 0; matrix products, arithmetic and copies ran while one was open for 0% -> 0% of each run, Pallas kernels for 7% -> 7%
where the time goes in v2:
time: 56.1 us; the launch traced here: 55.8 us
  blocking collectives  34.8 us (62%)
  Pallas kernels  10.7 us (19%)
  starting transfers between devices  9.42 us (17%)
  between operations  0.72 us (1%)
    all_to_all x2, blocking collectives, sent_to_all(): lax.all_to_all(jnp.broadcast_to(x[None], (peers, *x.shape)), axes, 0, 0,...  34.8 us
    ppermute x1, starting transfers between devices, shards(): got1 = lax.ppermute(own[1], SLAB, pairs)  4.83 us
    ppermute x1, starting transfers between devices, shards(): got0 = lax.ppermute(own[0], SLAB, across)  4.58 us
    pallas_call x1, Pallas kernels, finish(): pl.pallas_call(finish_kernel, out_shape=(jax.ShapeDtypeStruct((NV, NX, NY...  4.36 us
    pallas_call x1, Pallas kernels, main(): pl.pallas_call(main_kernel, out_shape=(jax.ShapeDtypeStruct((512, 1536),...  4.03 us
    pallas_call x1, Pallas kernels, edge(): pl.pallas_call(edge_kernel, out_shape=(jax.ShapeDtypeStruct((512, 512), B...  1.17 us
    pallas_call x1, Pallas kernels, pack(): pl.pallas_call(pack_kernel, out_shape=(plane, plane, jax.ShapeDtypeStruct...  1.14 us
  transfers between devices with their start and end apart: 2, of which 0 were waited for; matrix products, arithmetic and copies ran while one was open for 0% of the time, Pallas kernels for 7%

profile of v2, /device:TPU:1, one launch (start us, length us, event | category | flops | bytes accessed | tf_op | source)
XLA Modules:
  0.0 55.8 jit_solution(4497375769529773997)
XLA Ops:
  0.6 0.0 copy-start
  0.6 1.1 %pack.1 = (f32[17,16,128]{2,1,0:T(8,128)S(1)}, f32[17,16,128]{2,1,0:T(8,128)S(1)}, f32[3,8,16,128]{3,2,1,0:T(8,128)S(1)}) custom-call(s32[1]{0:T(128)} %bitcast.core, f32[8]{0:T(128)} %dens_ref.1, f32[8]{0:T(128)} %stiff_ref.1, f32[8]{0:T(128)} %damp_ref.1, f32[16,8,16,128]{3,2,1,0:T(8,128)} %v_ref.3, s32[8,16,128]{2,1,0:T(8,128)} %region_ref.1), custom_call_target="tpu_custom_call" | custom-call | flops 262144 | bytes 524288 | tf_op jit(solution)/shard_map/pack/pallas_call | solution.py:60
  1.8 4.6 %collective-permute-start = (f32[17,16,128]{2,1,0:T(8,128)S(1)}, f32[17,16,128]{2,1,0:T(8,128)S(1)}, u32[]{:S(2)}, u32[]{:S(2)}) collective-permute-start(f32[17,16,128]{2,1,0:T(8,128)S(1)} %get-tuple-element.16.own0), channel_id=1, source_target_pairs={{1,2},{2,1},{3,4},{4,3},{5,6},{6,5},{7,8},{8,7},{9,10},{10,9},{11,... | collective-permute-start | bytes 417800 | tf_op jit(solution)/shard_map/ppermute | solution.py:317
  6.4 4.8 %collective-permute-start.1 = (f32[17,16,128]{2,1,0:T(8,128)S(1)}, f32[17,16,128]{2,1,0:T(8,128)S(1)}, u32[]{:S(2)}, u32[]{:S(2)}) collective-permute-start(f32[17,16,128]{2,1,0:T(8,128)S(1)} %get-tuple-element.17.own1), channel_id=1, source_target_pairs={{0,1},{1,0},{2,3},{3,2},{4,5},{5,4},{6,7},{7,6},{8,9},{9,8},{10,11... | collective-permute-start | bytes 417800 | tf_op jit(solution)/shard_map/ppermute | solution.py:318
  11.2 0.0 copy-done
  11.2 4.0 %main.1 = (bf16[512,1536]{1,0:T(8,128)(2,1)S(1)}, f32[2,16,16,128]{3,2,1,0:T(8,128)S(1)}, f32[256,256]{1,0:T(8,128)S(1)}, f32[256,256]{1,0:T(8,128)S(1)}) custom-call(f32[16,8,16,128]{3,2,1,0:T(8,128)S(1)} %copy-done, f32[3,8,16,128]{3,2,1,0:T(8,128)S(1)} %get-tuple-element.12.fields, f32[16,8,16,128]{3,2,1,0:T(8,128)} %comp_hbm.1), custom_call_target="tpu_custom_call" | custom-call | flops 268435456 | bytes 5242880 | tf_op jit(solution)/shard_map/main/pallas_call | solution.py:169
  15.3 0.0 collective-permute-done.got0
  15.3 0.0 collective-permute-done.1.got1
  15.3 1.2 %edge.1 = (bf16[512,512]{1,0:T(8,128)(2,1)S(1)}, f32[8,128]{1,0:T(8,128)S(1)}) custom-call(s32[1]{0:T(128)} %bitcast.core, f32[2,16,16,128]{3,2,1,0:T(8,128)S(1)} %get-tuple-element.13.edge_ref, f32[256,256]{1,0:T(8,128)S(1)} %get-tuple-element.14.hh_ref, f32[256,256]{1,0:T(8,128)S(1)} %get-tuple-element.15.hl_ref, ...), custom_call_target="tpu_custom_call" | custom-call | flops 134217728 | bytes 2097152 | tf_op jit(solution)/shard_map/edge/pallas_call | solution.py:226
  16.5 0.1 broadcast_in_dim.14
  16.5 14.8 %all_to_all.10 = f32[32,1,1024]{2,1,0:T(1,128)S(1)} all-to-all(f32[32,1,1024]{2,1,0:T(1,128)S(1)} %broadcast_in_dim.14), channel_id=1, replica_groups=mesh['slab_0'=8,'slab_1'=4,'slab_2'=8,'slab_3'=2] {'slab_1','slab_2'}, dimensions={0} | all-to-all | bytes 262144 | tf_op jit(solution)/shard_map/all_to_all | solution.py:308
  31.4 0.1 reduce_sum.9
  31.5 19.9 %all_to_all.11 = f32[16,1,1024]{2,1,0:T(1,128)S(1)} all-to-all(f32[16,1,1024]{2,1,0:T(1,128)S(1)} %broadcast_in_dim.15), channel_id=1, replica_groups=mesh['slab_0'=8,'slab_1'=4,'slab_2'=8,'slab_3'=2] {'slab_0','slab_3'}, dimensions={0} | all-to-all | bytes 131072 | tf_op jit(solution)/shard_map/all_to_all | solution.py:308
  51.5 4.4 %finish.1 = (f32[16,8,16,128]{3,2,1,0:T(8,128)}, f32[16,16]{1,0:T(8,128)}, f32[16,16]{1,0:T(8,128)}) custom-call(f32[16,8,128]{2,1,0:T(8,128)S(1)} %bitcast.3, bf16[512,1536]{1,0:T(8,128)(2,1)S(1)} %get-tuple-element.19.xi_ref, bf16[512,512]{1,0:T(8,128)(2,1)S(1)} %get-tuple-element.20.xe_ref), custom_call_target="tpu_custom_call" | custom-call | flops 536870912 | bytes 3145728 | tf_op jit(solution)/shard_map/finish/pallas_call | solution.py:290
  (1 shorter events, 0.0 us)
Async XLA Ops:
  0.6 10.6 %copy-start = (f32[16,8,16,128]{3,2,1,0:T(8,128)S(1)}, f32[16,8,16,128]{3,2,1,0:T(8,128)}, u32[]{:S(2)}) copy-start(f32[16,8,16,128]{3,2,1,0:T(8,128)} %v_ref.3) | copy-start | bytes 3145732
  1.8 13.5 %collective-permute-start = (f32[17,16,128]{2,1,0:T(8,128)S(1)}, f32[17,16,128]{2,1,0:T(8,128)S(1)}, u32[]{:S(2)}, u32[]{:S(2)}) collective-permute-start(f32[17,16,128]{2,1,0:T(8,128)S(1)} %get-tuple-element.16.own0), channel_id=1, source_target_pairs={{1,2},{2,1},{3,4},{4,3},{5,6},{6,5},{7,8},{8,7},{9,10},{10,9},{11,... | collective-permute-start | bytes 417800 | tf_op jit(solution)/shard_map/ppermute | solution.py:317
  6.4 8.9 %collective-permute-start.1 = (f32[17,16,128]{2,1,0:T(8,128)S(1)}, f32[17,16,128]{2,1,0:T(8,128)S(1)}, u32[]{:S(2)}, u32[]{:S(2)}) collective-permute-start(f32[17,16,128]{2,1,0:T(8,128)S(1)} %get-tuple-element.17.own1), channel_id=1, source_target_pairs={{0,1},{1,0},{2,3},{3,2},{4,5},{5,4},{6,7},{7,6},{8,9},{9,8},{10,11... | collective-permute-start | bytes 417800 | tf_op jit(solution)/shard_map/ppermute | solution.py:318

commit v3 on v2

--- a/solution.py
+++ b/solution.py
@@ -12,7 +12,6 @@
 NV, NX, NY, NZ, NR = 16, 8, 16, 128, 8
 CELLS = 4096 * 16 * 128
 F32, BF16 = jnp.float32, jnp.bfloat16
-UNROLL = 4
 SMEM = pl.BlockSpec(memory_space=pltpu.SMEM)
 VMEM = pl.BlockSpec(memory_space=pltpu.VMEM)
 
@@ -29,7 +28,7 @@
     return [pltpu.with_memory_space_constraint(a, pltpu.HBM) for a in arrays]
 
 
-def pack_kernel(core, dens_ref, stiff_ref, damp_ref, v_ref, region_ref, out0, out1, fields, tables, regions, sems):
+def pack_kernel(core, dens_ref, stiff_ref, damp_ref, v_ref, region_ref, comp_ref, out0, out1, fields, tables, regions, sems):
     outs = (out0, out1)
     at = ((NX - 1) * core[0], (NX - 1) * (1 - core[0]))
     whole = pltpu.make_async_copy(region_ref, regions, sems.at[0])
@@ -55,12 +54,12 @@
         copy.wait()
 
 
-def pack(core, dens, stiff, dampt, basis, region):
+def pack(core, dens, stiff, dampt, basis, region, companion):
     plane = jax.ShapeDtypeStruct((NV + 1, NY, NZ), F32)
     return pl.pallas_call(
         pack_kernel,
         out_shape=(plane, plane, jax.ShapeDtypeStruct((3, NX, NY, NZ), F32)),
-        in_specs=[SMEM] + [HBM] * 5,
+        in_specs=[SMEM] + [HBM] * 6,
         out_specs=(VMEM,) * 3,
         scratch_shapes=[
             pltpu.SMEM((3, NR), F32),
@@ -70,17 +69,24 @@
         compiler_params=pltpu.CompilerParams(vmem_limit_bytes=4 << 20),
         cost_estimate=pl.CostEstimate(flops=1 << 18, bytes_accessed=1 << 19, transcendentals=0),
         name="pack",
-    )(core, *in_hbm(dens, stiff, dampt, basis, region))
+    )(core, *in_hbm(dens, stiff, dampt, basis, region, companion))
+
+
+def exact(left, right, dims=((1,), (0,))):
+    return lax.dot_general(left, right, (dims, ((), ())), precision=lax.Precision.HIGHEST, preferred_element_type=F32)
+
+
+def iota(shape, axis):
+    return lax.broadcasted_iota(jnp.int32, shape, axis)
+
+
+def ones_where(condition):
+    return jnp.where(condition, 1.0, 0.0).astype(F32)
 
 
 def folded(full):
-    rows = lax.broadcasted_iota(jnp.int32, (256, 256), 0)
-    cols = lax.broadcasted_iota(jnp.int32, (256, 256), 1)
-    kept = jnp.where(rows % 8 == cols % 8, full, 0.0)
-    by_row = jnp.sum(kept.reshape(32, 8, 256), axis=1)
-    pick = lax.broadcasted_iota(jnp.int32, (256, 128), 0) // 8
-    lane = lax.broadcasted_iota(jnp.int32, (256, 128), 1)
-    return jnp.dot(by_row, jnp.where(pick == lane, 1.0, 0.0).astype(F32), precision=lax.Precision.HIGHEST)
+    kept = jnp.where(iota((256, 256), 0) % 8 == iota((256, 256), 1) % 8, full, 0.0)
+    return jnp.sum(kept.reshape(32, 8, 256), axis=1)
 
 
 def products(high, low):
@@ -90,11 +96,8 @@
     return hh, hl
 
 
-def main_kernel(v_ref, fields, comp_hbm, x_ref, edge_ref, hh_ref, hl_ref, comp_ref, sems):
-    order = (*range(1, NX - 1), 0, NX - 1)
-    copies = {x: pltpu.make_async_copy(comp_hbm.at[:, x], comp_ref.at[:, x], sems.at[x]) for x in order}
-    for x in order:
-        copies[x].start()
+def main_kernel(v_ref, fields, comp_ref, x_ref, edge_ref, hh_ref, hl_ref):
+    order = (0, NX - 1, *range(1, NX - 1))
     yi = lax.broadcasted_iota(jnp.int32, (NY, NZ), 0)
     zi = lax.broadcasted_iota(jnp.int32, (NY, NZ), 1)
     for x in range(1, NX - 1):
@@ -110,7 +113,7 @@
                 x_ref[pl.ds(rows + 384, 16), cols] = vl
             return carry
 
-        lax.fori_loop(0, NV // 2, split, 0, unroll=UNROLL)
+        lax.fori_loop(0, NV // 2, split, 0, unroll=True)
     for x in order:
         c = fields[0, x]
         diag = -fields[1, x]
@@ -137,7 +140,6 @@
                 f = f - b * pltpu.roll(v, shift, axis)
             return f
 
-        copies[x].wait()
         if 0 < x < NX - 1:
 
             def pair(p, carry, x=x, one=one):
@@ -151,7 +153,7 @@
                     x_ref[pl.ds(rows + 256, 16), cols] = fl
                 return carry
 
-            lax.fori_loop(0, NV // 2, pair, 0, unroll=UNROLL)
+            lax.fori_loop(0, NV // 2, pair, 0, unroll=True)
         else:
             e = 0 if x == 0 else 1
 
@@ -159,7 +161,7 @@
                 edge_ref[e, i] = one(i)
                 return carry
 
-            lax.fori_loop(0, NV, single, 0, unroll=UNROLL)
+            lax.fori_loop(0, NV, single, 0, unroll=True)
     hh, hl = products(x_ref[0:256], x_ref[256:512])
     hh_ref[...] = hh
     hl_ref[...] = hl
@@ -174,16 +176,15 @@
             jax.ShapeDtypeStruct((256, 256), F32),
             jax.ShapeDtypeStruct((256, 256), F32),
         ),
-        in_specs=[VMEM, VMEM, HBM],
+        in_specs=[VMEM] * 3,
         out_specs=(VMEM,) * 4,
-        scratch_shapes=[pltpu.VMEM((NV, NX, NY, NZ), F32), pltpu.SemaphoreType.DMA((NX,))],
         compiler_params=pltpu.CompilerParams(vmem_limit_bytes=16 << 20),
         cost_estimate=pl.CostEstimate(flops=1 << 28, bytes_accessed=5 << 20, transcendentals=0),
         name="main",
-    )(basis, fields, *in_hbm(companion))
-
-
-def edge_kernel(core, edge_ref, hh_ref, hl_ref, own0, own1, got0, got1, x_ref, out_ref):
+    )(basis, fields, companion)
+
+
+def edge_kernel(core, edge_ref, hh_ref, hl_ref, own0, own1, got0, got1, xi_ref, x_ref, out_ref, kept_ref):
     upper = (core[0], 1 - core[0])
     for side, (own, got) in enumerate(((own0, got0), (own1, got1))):
         place = upper[side]
@@ -212,53 +213,82 @@
     hh, hl = products(x_ref[0:256], x_ref[256:512])
     same = folded(hh + hh_ref[...])
     mixed = folded(hl + hl_ref[...])
-    eye = jnp.where(
-        lax.broadcasted_iota(jnp.int32, (32, 128), 0) == lax.broadcasted_iota(jnp.int32, (32, 128), 1), 1.0, 0.0
-    ).astype(F32)
-    turned = lax.dot_general(eye, mixed, (((1,), (1,)), ((), ())), precision=lax.Precision.HIGHEST)
-    turned = jnp.pad(turned, ((0, 0), (0, 96)))
-    total = (same + mixed + turned) * (1.0 / CELLS)
-    lanes = total[16:32] + pltpu.roll(total[0:16], 32, 1)
-    out_ref[...] = lanes[0:8] + pltpu.roll(lanes[8:16], 64, 1)
-
-
-def edge(core, edges, hh, hl, own, got):
+    both = same + mixed
+    repeat = ones_where(iota((128, 128), 0) // 8 == iota((128, 128), 1) % NV)
+    square = exact(mixed, ones_where(iota((256, 128), 0) // 8 == iota((256, 128), 1)))
+    group, lane = iota((32, 128), 0), iota((32, 128), 1)
+    tiles = [
+        exact(both[:, 128 * k : 128 * k + 128], repeat)
+        + exact(square, ones_where(group - NV * k == lane % NV), ((0,), (0,)))[0:32]
+        for k in (0, 1)
+    ]
+    row, lane = iota((NV, 128), 0), iota((NV, 128), 1)
+    fv, ff, vv = tiles[1][0:NV], tiles[0][0:NV], tiles[1][NV:32]
+    sums = []
+    for m in (fv, jnp.where(lane % NV >= row, ff, vv)):
+        m = jnp.where(lane // NV == row % 8, m, 0.0)
+        sums += [jnp.sum(m[0:8], axis=0, keepdims=True), jnp.sum(m[8:16], axis=0, keepdims=True)]
+    sums.append(jnp.sum(jnp.where(lane == row, vv, 0.0), axis=0, keepdims=True))
+    for k, m in enumerate(sums):
+        out_ref[k : k + 1] = m * (1.0 / CELLS)
+
+
+def edge(core, edges, hh, hl, own, got, xi):
     return pl.pallas_call(
         edge_kernel,
-        out_shape=(jax.ShapeDtypeStruct((512, 512), BF16), jax.ShapeDtypeStruct((8, 128), F32)),
-        in_specs=[SMEM] + [VMEM] * 7,
-        out_specs=(VMEM, VMEM),
+        out_shape=(
+            jax.ShapeDtypeStruct((512, 512), BF16),
+            jax.ShapeDtypeStruct((5, 128), F32),
+            jax.ShapeDtypeStruct(xi.shape, xi.dtype),
+        ),
+        in_specs=[SMEM] + [VMEM] * 7 + [pl.BlockSpec(memory_space=pl.ANY)],
+        out_specs=(VMEM, VMEM, pl.BlockSpec(memory_space=pl.ANY)),
+        input_output_aliases={8: 2},
         compiler_params=pltpu.CompilerParams(vmem_limit_bytes=8 << 20),
         cost_estimate=pl.CostEstimate(flops=1 << 27, bytes_accessed=2 << 20, transcendentals=0),
         name="edge",
-    )(core, edges, hh, hl, *own, *got)
+    )(core, edges, hh, hl, *own, *got, xi)
 
 
 def finish_kernel(parts_ref, xi_ref, xe_ref, new_ref, proj_ref, r_ref, stage, sems):
-    packed = jnp.sum(parts_ref[...], axis=0)
-    lanes = jnp.concatenate([packed, pltpu.roll(packed, 64, 1)], axis=0)
-    vf, vv, ff, fv = (lanes[:, 16 * k : 16 * k + 16] for k in range(4))
+    row, lane = iota((NV, 128), 0), iota((NV, 128), 1)
+    total = [jnp.sum(parts_ref[pl.ds(k, parts_ref.shape[0] // 5, stride=5), :], axis=0, keepdims=True) for k in range(5)]
+    mine = lane // NV == row % 8
+    spread_out = [
+        jnp.where(mine, jnp.where(row < 8, jnp.broadcast_to(lo, (NV, 128)), jnp.broadcast_to(hi, (NV, 128))), 0.0)
+        for lo, hi in ((total[0], total[1]), (total[2], total[3]))
+    ]
+    spread_out = jnp.concatenate(spread_out, axis=0)
+    source, target = iota((128, 128), 0), iota((128, 128), 1)
+    squares = exact(spread_out, ones_where((source % NV == target % NV) & (target // NV % 2 == 0) & (target < 48)))
+    turned = exact(ones_where(lane % NV == row), spread_out, ((1,), (1,)))
+    fv, mixed = squares[0:NV, 0:NV], squares[NV:32, 0:NV]
+    vf, mixed_t = turned[:, 0:NV], turned[:, NV:32]
+    r, c = iota((NV, NV), 0), iota((NV, NV), 1)
+    ff = jnp.where(c >= r, mixed, mixed_t)
+    own = jnp.broadcast_to(total[4], (NV, 128))[:, 0:NV]
+    vv = jnp.where(c < r, mixed, jnp.where(c > r, mixed_t, own))
     proj_ref[...] = vf
-    exact = functools.partial(jnp.dot, precision=lax.Precision.HIGHEST, preferred_element_type=F32)
     gram = ff + exact(fv, exact(vv, vf) - 2.0 * vf)
-    row = lax.broadcasted_iota(jnp.int32, (NV, 128), 0)
-    lane = lax.broadcasted_iota(jnp.int32, (NV, 128), 1)
-    unit = jnp.where(row + 16 == lane, 1.0, 0.0).astype(F32)
-    shifted_fv = jnp.where((lane >= 32) & (lane < 48), pltpu.roll(lanes, 128 - 16, 1), 0.0)
-    a = jnp.pad(gram, ((0, 0), (0, 112))) + unit + shifted_fv
-    for k in range(NV - 1):
-        col = jnp.broadcast_to(a[:, k : k + 1], (NV, 128))
-        pivot = jnp.broadcast_to(col[k : k + 1], (NV, 128))
-        factor = jnp.where(row > k, col / pivot, 0.0)
-        a = a - factor * jnp.broadcast_to(a[k : k + 1], (NV, 128))
+    unit = ones_where(row + 16 == lane)
+    a = jnp.pad(gram, ((0, 0), (0, 112))) + unit + jnp.where(lane >= 32, squares[0:NV], 0.0)
+    for k in range(0, NV - 2, 2):
+        col0, col1 = (jnp.broadcast_to(a[:, k + j : k + j + 1], (NV, 128)) for j in (0, 1))
+        row0, row1 = (jnp.broadcast_to(a[k + j : k + j + 1], (NV, 128)) for j in (0, 1))
+        p, q, t = (jnp.broadcast_to(m, (NV, 128)) for m in (col0[k : k + 1], col1[k : k + 1], col1[k + 1 : k + 2]))
+        scale = jnp.where(row > k + 1, 1.0 / (p * t - q * q), 0.0)
+        a = a - ((col0 * t - col1 * q) * scale) * row0 - ((col1 * p - col0 * q) * scale) * row1
+    above = pltpu.roll(a, 1, 0)
+    below_pivot, pivot = (jnp.sum(jnp.where(lane == row - 1, m, 0.0), axis=1, keepdims=True) for m in (a, above))
+    odd = row % 2 == 1
+    a = a - jnp.where(odd, below_pivot / jnp.where(odd[:, 0:1], pivot, 1.0), 0.0) * above
     pivots = jnp.sum(jnp.where(row == lane, a, 0.0), axis=1, keepdims=True)
     a = a / jnp.sqrt(pivots)
     r_ref[...] = jnp.where(lane >= row, a, 0.0)[:, 0:NV]
     w = jnp.where(lane < 32, a, -a)
     w = jnp.broadcast_to(w[:, None, :], (NV, 8, 128)).reshape(128, 128)
     wh, wl = two_parts(w)
-    source = lax.broadcasted_iota(jnp.int32, (128, 256), 0)
-    target = lax.broadcasted_iota(jnp.int32, (128, 256), 1)
+    source, target = iota((128, 256), 0), iota((128, 256), 1)
     spread = jnp.where(source - 16 == target // 8, 1.0, 0.0).astype(BF16)
     keep = source % 8 == target % 8
     kh, kl = (
@@ -277,11 +307,9 @@
         got = planes(xe_ref, 0 if x == 0 else 1) if x in (0, NX - 1) else planes(xi_ref, x - 1)
         for h in range(2):
             stage[:, x, 8 * h : 8 * h + 8, :] = got[:, NZ * h : NZ * h + NZ].reshape(NV, 8, NZ)
-        if x % 2:
-            pair = pl.ds(x - 1, 2)
-            copy = pltpu.make_async_copy(stage.at[:, pair], new_ref.at[:, pair], sems.at[x // 2])
-            copy.start()
-            copies.append(copy)
+        copy = pltpu.make_async_copy(stage.at[:, x], new_ref.at[:, x], sems.at[x])
+        copy.start()
+        copies.append(copy)
     for copy in copies:
         copy.wait()
 
@@ -296,7 +324,7 @@
         ),
         in_specs=[VMEM] * 3,
         out_specs=(pl.BlockSpec(memory_space=pl.ANY), VMEM, VMEM),
-        scratch_shapes=[pltpu.VMEM((NV, NX, NY, NZ), F32), pltpu.SemaphoreType.DMA((NX // 2,))],
+        scratch_shapes=[pltpu.VMEM((NV, NX, NY, NZ), F32), pltpu.SemaphoreType.DMA((NX,))],
         compiler_params=pltpu.CompilerParams(vmem_limit_bytes=16 << 20),
         cost_estimate=pl.CostEstimate(flops=1 << 29, bytes_accessed=3 << 20, transcendentals=0),
         name="finish",
@@ -311,16 +339,16 @@
 def shards(krylov_basis_block, companion, region, inv_density, stiffness, damping):
     core = lax.axis_index("slab_3").astype(jnp.int32).reshape(1)
     count = lax.axis_size(SLAB)
-    *own, fields = pack(core, inv_density, stiffness, damping, krylov_basis_block, region)
+    *own, fields = pack(core, inv_density, stiffness, damping, krylov_basis_block, region, companion)
     pairs = [(i, i ^ 1) for i in range(count)]
     across = [(i, i + 1 if i % 2 else i - 1) for i in range(1, count - 1)]
     got0 = lax.ppermute(own[0], SLAB, across)
     got1 = lax.ppermute(own[1], SLAB, pairs)
     xi, edges, hh, hl = main(krylov_basis_block, fields, companion)
-    xe, packed = edge(core, edges, hh, hl, own, (got0, got1))
-    near = sent_to_all(packed.reshape(1, 1024), ("slab_1", "slab_2")).sum(axis=0)
-    far = sent_to_all(near.reshape(1, 1024), ("slab_0", "slab_3"))
-    new_block, projection, rfactor = finish(far.reshape(-1, 8, 128), xi, xe)
+    xe, packed, xi = edge(core, edges, hh, hl, own, (got0, got1), xi)
+    near = sent_to_all(packed.reshape(1, 640), ("slab_1", "slab_2")).sum(axis=0)
+    far = sent_to_all(near.reshape(1, 640), ("slab_0", "slab_3"))
+    new_block, projection, rfactor = finish(far.reshape(-1, 128), xi, xe)
     return new_block, projection, rfactor
 
 

time: 56.1 us -> 53.6 us (0.955)
  Pallas kernels: 10.7 us -> 7.48 us
  blocking collectives: 34.8 us -> 35.6 us
    pallas_call x1, Pallas kernels: 4.03 us -> 1.41 us  [main(): pl.pallas_call(main_kernel, out_shape=(jax.ShapeDtypeStruct((512, 1536),...]
    all_to_all x2, blocking collectives: 34.8 us -> 35.6 us  [sent_to_all(): lax.all_to_all(jnp.broadcast_to(x[None], (peers, *x.shape)), axes, 0, 0,...]
    pallas_call x1, Pallas kernels: 4.36 us -> 3.6 us  [finish(): pl.pallas_call(finish_kernel, out_shape=(jax.ShapeDtypeStruct((NV, NX, NY...]
  transfers between devices with their start and end apart: 2 -> 2, of which waited for: 0 -> 0; matrix products, arithmetic and copies ran while one was open for 0% -> 0% of each run, Pallas kernels for 7% -> 3%
where the time goes in v3:
time: 53.6 us; the launch traced here: 53.4 us
  blocking collectives  35.6 us (66%)
  starting transfers between devices  9.42 us (18%)
  Pallas kernels  7.48 us (14%)
  between operations  0.73 us (1%)
    all_to_all x2, blocking collectives, sent_to_all(): lax.all_to_all(jnp.broadcast_to(x[None], (peers, *x.shape)), axes, 0, 0,...  35.6 us
    ppermute x1, starting transfers between devices, shards(): got1 = lax.ppermute(own[1], SLAB, pairs)  4.83 us
    ppermute x1, starting transfers between devices, shards(): got0 = lax.ppermute(own[0], SLAB, across)  4.58 us
    pallas_call x1, Pallas kernels, finish(): pl.pallas_call(finish_kernel, out_shape=(jax.ShapeDtypeStruct((NV, NX, NY...  3.6 us
    pallas_call x1, Pallas kernels, main(): pl.pallas_call(main_kernel, out_shape=(jax.ShapeDtypeStruct((512, 1536),...  1.41 us
    pallas_call x1, Pallas kernels, edge(): pl.pallas_call(edge_kernel, out_shape=(jax.ShapeDtypeStruct((512, 512), B...  1.26 us
    pallas_call x1, Pallas kernels, pack(): pl.pallas_call(pack_kernel, out_shape=(plane, plane, jax.ShapeDtypeStruct...  1.2 us
  transfers between devices with their start and end apart: 2, of which 0 were waited for; matrix products, arithmetic and copies ran while one was open for 0% of the time, Pallas kernels for 3%

profile of v3, /device:TPU:1, one launch (start us, length us, event | category | flops | bytes accessed | tf_op | source)
XLA Modules:
  0.0 53.4 jit_solution(500962643649639554)
XLA Ops:
  0.6 0.0 copy-start
  0.6 0.0 copy-start.1
  0.7 1.2 %pack.1 = (f32[17,16,128]{2,1,0:T(8,128)S(1)}, f32[17,16,128]{2,1,0:T(8,128)S(1)}, f32[3,8,16,128]{3,2,1,0:T(8,128)S(1)}) custom-call(s32[1]{0:T(128)} %bitcast.core, f32[8]{0:T(128)} %dens_ref.1, f32[8]{0:T(128)} %stiff_ref.1, f32[8]{0:T(128)} %damp_ref.1, f32[16,8,16,128]{3,2,1,0:T(8,128)} %v_ref.3, s32[8,16,128]{2,1,0:T(8,128)} %region_ref.1, ...), custom_call_target="tpu_custom_call" | custom-call | flops 262144 | bytes 524288 | tf_op jit(solution)/shard_map/pack/pallas_call | solution.py:59
  1.9 4.6 %collective-permute-start = (f32[17,16,128]{2,1,0:T(8,128)S(1)}, f32[17,16,128]{2,1,0:T(8,128)S(1)}, u32[]{:S(2)}, u32[]{:S(2)}) collective-permute-start(f32[17,16,128]{2,1,0:T(8,128)S(1)} %get-tuple-element.17.own0), channel_id=1, source_target_pairs={{1,2},{2,1},{3,4},{4,3},{5,6},{6,5},{7,8},{8,7},{9,10},{10,9},{11,... | collective-permute-start | bytes 417800 | tf_op jit(solution)/shard_map/ppermute | solution.py:345
  6.5 4.8 %collective-permute-start.1 = (f32[17,16,128]{2,1,0:T(8,128)S(1)}, f32[17,16,128]{2,1,0:T(8,128)S(1)}, u32[]{:S(2)}, u32[]{:S(2)}) collective-permute-start(f32[17,16,128]{2,1,0:T(8,128)S(1)} %get-tuple-element.18.own1), channel_id=1, source_target_pairs={{0,1},{1,0},{2,3},{3,2},{4,5},{5,4},{6,7},{7,6},{8,9},{9,8},{10,11... | collective-permute-start | bytes 417800 | tf_op jit(solution)/shard_map/ppermute | solution.py:346
  11.3 0.0 copy-done
  11.3 0.0 copy-done.1
  11.3 1.4 %main.1 = (bf16[512,1536]{1,0:T(8,128)(2,1)S(1)}, f32[2,16,16,128]{3,2,1,0:T(8,128)S(1)}, f32[256,256]{1,0:T(8,128)S(1)}, f32[256,256]{1,0:T(8,128)S(1)}) custom-call(f32[16,8,16,128]{3,2,1,0:T(8,128)S(1)} %copy-done, f32[3,8,16,128]{3,2,1,0:T(8,128)S(1)} %get-tuple-element.13.fields, f32[16,8,16,128]{3,2,1,0:T(8,128)S(1)} %copy-done.1), custom_call_target="tpu_custom_call" | custom-call | flops 268435456 | bytes 5242880 | tf_op jit(solution)/shard_map/main/pallas_call | solution.py:171
  12.7 0.0 collective-permute-done.got0
  12.7 0.0 collective-permute-done.1.got1
  12.7 1.3 %edge.1 = (bf16[512,512]{1,0:T(8,128)(2,1)S(1)}, f32[5,128]{1,0:T(8,128)S(1)}, bf16[512,1536]{1,0:T(8,128)(2,1)S(1)}) custom-call(s32[1]{0:T(128)} %bitcast.core, f32[2,16,16,128]{3,2,1,0:T(8,128)S(1)} %get-tuple-element.14.edge_ref, f32[256,256]{1,0:T(8,128)S(1)} %get-tuple-element.15.hh_ref, ...), custom_call_target="tpu_custom_call", output_to_operand_aliasing={{2}: (8, {})} | custom-call | flops 134217728 | bytes 2097152 | tf_op jit(solution)/shard_map/edge/pallas_call | solution.py:237
  14.1 16.3 %all_to_all.10 = f32[32,1,640]{2,1,0:T(1,128)S(1)} all-to-all(f32[32,1,640]{2,1,0:T(1,128)S(1)} %broadcast_in_dim.14), channel_id=1, replica_groups=mesh['slab_0'=8,'slab_1'=4,'slab_2'=8,'slab_3'=2] {'slab_1','slab_2'}, dimensions={0} | all-to-all | bytes 163840 | tf_op jit(solution)/shard_map/all_to_all | solution.py:336
  30.4 0.1 reduce_sum.9
  30.5 19.3 %all_to_all.11 = f32[16,1,640]{2,1,0:T(1,128)S(1)} all-to-all(f32[16,1,640]{2,1,0:T(1,128)S(1)} %broadcast_in_dim.15), channel_id=1, replica_groups=mesh['slab_0'=8,'slab_1'=4,'slab_2'=8,'slab_3'=2] {'slab_0','slab_3'}, dimensions={0} | all-to-all | bytes 81920 | tf_op jit(solution)/shard_map/all_to_all | solution.py:336
  49.8 3.6 %finish.1 = (f32[16,8,16,128]{3,2,1,0:T(8,128)}, f32[16,16]{1,0:T(8,128)}, f32[16,16]{1,0:T(8,128)}) custom-call(f32[80,128]{1,0:T(8,128)S(1)} %bitcast.3, bf16[512,1536]{1,0:T(8,128)(2,1)S(1)} %get-tuple-element.21.xi_ref, bf16[512,512]{1,0:T(8,128)(2,1)S(1)} %get-tuple-element.22.xe_ref), custom_call_target="tpu_custom_call" | custom-call | flops 536870912 | bytes 3145728 | tf_op jit(solution)/shard_map/finish/pallas_call | solution.py:318
  (2 shorter events, 0.1 us)
Async XLA Ops:
  0.6 10.7 %copy-start = (f32[16,8,16,128]{3,2,1,0:T(8,128)S(1)}, f32[16,8,16,128]{3,2,1,0:T(8,128)}, u32[]{:S(2)}) copy-start(f32[16,8,16,128]{3,2,1,0:T(8,128)} %v_ref.3) | copy-start | bytes 3145732
  0.6 10.7 %copy-start.1 = (f32[16,8,16,128]{3,2,1,0:T(8,128)S(1)}, f32[16,8,16,128]{3,2,1,0:T(8,128)}, u32[]{:S(2)}) copy-start(f32[16,8,16,128]{3,2,1,0:T(8,128)} %comp_ref.3) | copy-start | bytes 3145732
  1.9 10.9 %collective-permute-start = (f32[17,16,128]{2,1,0:T(8,128)S(1)}, f32[17,16,128]{2,1,0:T(8,128)S(1)}, u32[]{:S(2)}, u32[]{:S(2)}) collective-permute-start(f32[17,16,128]{2,1,0:T(8,128)S(1)} %get-tuple-element.17.own0), channel_id=1, source_target_pairs={{1,2},{2,1},{3,4},{4,3},{5,6},{6,5},{7,8},{8,7},{9,10},{10,9},{11,... | collective-permute-start | bytes 417800 | tf_op jit(solution)/shard_map/ppermute | solution.py:345
  6.5 6.3 %collective-permute-start.1 = (f32[17,16,128]{2,1,0:T(8,128)S(1)}, f32[17,16,128]{2,1,0:T(8,128)S(1)}, u32[]{:S(2)}, u32[]{:S(2)}) collective-permute-start(f32[17,16,128]{2,1,0:T(8,128)S(1)} %get-tuple-element.18.own1), channel_id=1, source_target_pairs={{0,1},{1,0},{2,3},{3,2},{4,5},{5,4},{6,7},{7,6},{8,9},{9,8},{10,11... | collective-permute-start | bytes 417800 | tf_op jit(solution)/shard_map/ppermute | solution.py:346

commit v4 on v3

v4 whole, which is shorter than its diff:
```python
import functools

import jax
import jax.numpy as jnp
from jax import lax
from jax.experimental import pallas as pl
from jax.experimental.pallas import tpu as pltpu
from jax.sharding import Mesh
from jax.sharding import PartitionSpec as P

SLAB = ("slab_0", "slab_1", "slab_2", "slab_3")
NV, NX, NY, NZ, NR = 16, 8, 16, 128, 8
CELLS = 4096 * 16 * 128
F32, BF16 = jnp.float32, jnp.bfloat16
SMEM = pl.BlockSpec(memory_space=pltpu.SMEM)
VMEM = pl.BlockSpec(memory_space=pltpu.VMEM)


def two_parts(x):
    high = x.astype(BF16)
    return high, (x - high.astype(F32)).astype(BF16)


HBM = pl.BlockSpec(memory_space=pltpu.HBM)


def in_hbm(*arrays):
    return [pltpu.with_memory_space_constraint(a, pltpu.HBM) for a in arrays]


def pack_kernel(core, dens_ref, stiff_ref, damp_ref, v_ref, region_ref, comp_ref, out0, out1, fields, tables, regions, sems):
    outs = (out0, out1)
    at = ((NX - 1) * core[0], (NX - 1) * (1 - core[0]))
    whole = pltpu.make_async_copy(region_ref, regions, sems.at[0])
    small = [
        pltpu.make_async_copy(ref, tables.at[k], sems.at[1 + k]) for k, ref in enumerate((dens_ref, stiff_ref, damp_ref))
    ]
    planes = [pltpu.make_async_copy(v_ref.at[:, at[k]], outs[k].at[pl.ds(0, NV)], sems.at[4 + k]) for k in (0, 1)]
    for copy in (whole, *small, *planes):
        copy.start()
    for copy in (*small, whole):
        copy.wait()
    for x in range(NX):
        region = regions[x]
        values = [jnp.zeros(region.shape, F32)] * 3
        for r in range(NR):
            here = region == r
            values = [jnp.where(here, tables[k, r], values[k]) for k in range(3)]
        for k in range(3):
            fields[k, x] = values[k]
    for k in (0, 1):
        outs[k][NV] = fields[0, at[k]]
    for copy in planes:
        copy.wait()


def pack(core, dens, stiff, dampt, basis, region, companion):
    plane = jax.ShapeDtypeStruct((NV + 1, NY, NZ), F32)
    return pl.pallas_call(
        pack_kernel,
        out_shape=(plane, plane, jax.ShapeDtypeStruct((3, NX, NY, NZ), F32)),
        in_specs=[SMEM] + [HBM] * 6,
        out_specs=(VMEM,) * 3,
        scratch_shapes=[
            pltpu.SMEM((3, NR), F32),
            pltpu.VMEM((NX, NY, NZ), jnp.int32),
            pltpu.SemaphoreType.DMA((6,)),
        ],
        compiler_params=pltpu.CompilerParams(vmem_limit_bytes=4 << 20),
        cost_estimate=pl.CostEstimate(flops=1 << 18, bytes_accessed=1 << 19, transcendentals=0),
        name="pack",
    )(core, *in_hbm(dens, stiff, dampt, basis, region, companion))


def exact(left, right, dims=((1,), (0,))):
    return lax.dot_general(left, right, (dims, ((), ())), precision=lax.Precision.HIGHEST, preferred_element_type=F32)


def iota(shape, axis):
    return lax.broadcasted_iota(jnp.int32, shape, axis)


def ones_where(condition):
    return jnp.where(condition, 1.0, 0.0).astype(F32)


def folded(full):
    rows, cols = full.shape
    kept = jnp.where(iota(full.shape, 0) % 8 == iota(full.shape, 1) % 8, full, 0.0)
    return jnp.sum(kept.reshape(rows // 8, 8, cols), axis=1)


def tiled(half):
    return exact(half, ones_where(iota((128, 128), 0) // 8 == iota((128, 128), 1) % NV))


def beside(square):
    return jnp.pad(square, ((16, 0), (128, 0)))


def times_turned(left, right):
    return lax.dot_general(left, right, (((1,), (1,)), ((), ())), preferred_element_type=F32)


def main_kernel(v_ref, fields, comp_ref, xf_ref, xv_ref, edge_ref, tiles_ref):
    yi = lax.broadcasted_iota(jnp.int32, (NY, NZ), 0)
    zi = lax.broadcasted_iota(jnp.int32, (NY, NZ), 1)
    for x in range(NX):
        for i in range(0, NV, 2):
            v0, v1 = v_ref[i, x], v_ref[i + 1, x]
            for h in range(2):
                cols, half = slice((2 * x + h) * NZ, (2 * x + h + 1) * NZ), slice(8 * h, 8 * h + 8)
                high, low = two_parts(jnp.concatenate([v0[half], v1[half]], axis=0))
                xv_ref[8 * i : 8 * i + 16, cols] = high
                xv_ref[128 + 8 * i : 144 + 8 * i, cols] = low
    for x in (0, NX - 1, *range(1, NX - 1)):
        c = fields[0, x]
        diag = -fields[1, x]
        damp = fields[2, x]
        xs = []
        for xn in (x - 1, x + 1):
            if 0 <= xn < NX:
                b = 0.5 * (c + fields[0, xn])
                diag = diag + b
                xs.append((xn, b))
        sides = []
        for shift, axis, end, at in ((NY - 1, 0, NY - 1, yi), (1, 0, 0, yi), (NZ - 1, 1, NZ - 1, zi), (1, 1, 0, zi)):
            outside = at == end
            b = jnp.where(outside, c, 0.5 * (c + pltpu.roll(c, shift, axis)))
            diag = diag + b
            sides.append((shift, axis, jnp.where(outside, 0.0, b)))

        def one(i, x=x, diag=diag, damp=damp, xs=xs, sides=sides):
            v = v_ref[i, x]
            f = diag * v + damp * comp_ref[i, x]
            for xn, b in xs:
                f = f - b * v_ref[i, xn]
            for shift, axis, b in sides:
                f = f - b * pltpu.roll(v, shift, axis)
            return f

        if x in (0, NX - 1):
            for i in range(NV):
                edge_ref[x // (NX - 1), i] = one(i)
            continue
        for i in range(0, NV, 2):
            f0, f1 = one(i), one(i + 1)
            for h in range(2):
                at = 2 * (x - 1) + h
                cols, half = slice(at * NZ, (at + 1) * NZ), slice(8 * h, 8 * h + 8)
                high, low = two_parts(jnp.concatenate([f0[half], f1[half]], axis=0))
                xf_ref[8 * i : 8 * i + 16, cols] = high
                xf_ref[128 + 8 * i : 144 + 8 * i, cols] = low
    inner, ends = slice(2 * NZ, 14 * NZ), (slice(0, 2 * NZ), slice(14 * NZ, 16 * NZ))
    high, low = (jnp.concatenate([xf_ref[k : k + 128], xv_ref[k : k + 128, inner]], axis=0) for k in (0, 128))
    end_high, end_low = (jnp.concatenate([xv_ref[k : k + 128, e] for e in ends], axis=1) for k in (0, 128))
    same, mixed = (
        folded(times_turned(high, right)) + beside(folded(times_turned(end_high, end_right)))
        for right, end_right in ((high, end_high), (low, end_low))
    )
    both = same + mixed
    square = exact(mixed, ones_where(iota((256, 128), 0) // 8 == iota((256, 128), 1)))
    group, lane = iota((32, 128), 0), iota((32, 128), 1)
    over_f, over_v = (
        tiled(both[:, 128 * k : 128 * k + 128])
        + exact(square, ones_where(group - NV * k == lane % NV), ((0,), (0,)))[0:32]
        for k in (0, 1)
    )
    tiles_ref[0:NV] = over_f[0:NV]
    tiles_ref[NV : NV + 32] = over_v


def main(basis, fields, companion):
    return pl.pallas_call(
        main_kernel,
        out_shape=(
            jax.ShapeDtypeStruct((256, 1536), BF16),
            jax.ShapeDtypeStruct((256, 2048), BF16),
            jax.ShapeDtypeStruct((2, NV, NY, NZ), F32),
            jax.ShapeDtypeStruct((48, 128), F32),
        ),
        in_specs=[VMEM] * 3,
        out_specs=(VMEM,) * 4,
        compiler_params=pltpu.CompilerParams(vmem_limit_bytes=16 << 20),
        cost_estimate=pl.CostEstimate(flops=1 << 28, bytes_accessed=5 << 20, transcendentals=0),
        name="main",
    )(basis, fields, companion)


def edge_kernel(core, edge_ref, tiles_ref, xv_ref, own0, own1, got0, got1, xf_ref, xe_ref, out_ref, kept_ref):
    upper = (core[0], 1 - core[0])
    for side, (own, got) in enumerate(((own0, got0), (own1, got1))):
        place = upper[side]
        c, other = own[NV], got[NV]
        b = 0.5 * (c + jnp.where(other > 0.0, other, c))
        for i in range(0, NV, 2):
            f0, f1 = (edge_ref[place, k] + b * (own[k] - got[k]) for k in (i, i + 1))
            for h in range(2):
                cols, half = pl.ds(pl.multiple_of((place * 2 + h) * NZ, NZ), NZ), slice(8 * h, 8 * h + 8)
                high, low = two_parts(jnp.concatenate([f0[half], f1[half]], axis=0))
                xe_ref[8 * i : 8 * i + 16, cols] = high
                xe_ref[128 + 8 * i : 144 + 8 * i, cols] = low
    fh, fl = xe_ref[0:128], xe_ref[128:256]
    ends = (slice(0, 2 * NZ), slice(14 * NZ, 16 * NZ))
    vh, vl = (jnp.concatenate([xv_ref[k : k + 128, e] for e in ends], axis=1) for k in (0, 128))
    high, low = jnp.concatenate([fh, vh], axis=0), jnp.concatenate([fl, vl], axis=0)
    sums = folded(
        times_turned(jnp.concatenate([fh, fh, fl], axis=1), jnp.concatenate([high, low, high], axis=1))
    )
    ff = tiled(sums[:, 0:128]) + tiles_ref[0:NV]
    fv = tiled(sums[:, 128:256]) + tiles_ref[NV:32]
    vv = tiles_ref[32:48]
    row, lane = iota((NV, 128), 0), iota((NV, 128), 1)
    sums = []
    for m in (fv, jnp.where(lane % NV >= row, ff, vv)):
        m = jnp.where(lane // NV == row % 8, m, 0.0)
        sums += [jnp.sum(m[0:8], axis=0, keepdims=True), jnp.sum(m[8:16], axis=0, keepdims=True)]
    sums.append(jnp.sum(jnp.where(lane == row, vv, 0.0), axis=0, keepdims=True))
    for k, m in enumerate(sums):
        out_ref[k : k + 1] = m * (1.0 / CELLS)


def edge(core, edges, tiles, xv, own, got, xf):
    anywhere = pl.BlockSpec(memory_space=pl.ANY)
    return pl.pallas_call(
        edge_kernel,
        out_shape=(
            jax.ShapeDtypeStruct((256, 512), BF16),
            jax.ShapeDtypeStruct((5, 128), F32),
            jax.ShapeDtypeStruct(xf.shape, xf.dtype),
        ),
        in_specs=[SMEM] + [VMEM] * 7 + [anywhere],
        out_specs=(VMEM, VMEM, anywhere),
        input_output_aliases={8: 2},
        compiler_params=pltpu.CompilerParams(vmem_limit_bytes=8 << 20),
        cost_estimate=pl.CostEstimate(flops=1 << 27, bytes_accessed=2 << 20, transcendentals=0),
        name="edge",
    )(core, edges, tiles, xv, *own, *got, xf)


def finish_kernel(parts_ref, xf_ref, xe_ref, xv_ref, new_ref, proj_ref, r_ref, stage, sems):
    row, lane = iota((NV, 128), 0), iota((NV, 128), 1)
    total = [jnp.sum(parts_ref[pl.ds(k, parts_ref.shape[0] // 5, stride=5), :], axis=0, keepdims=True) for k in range(5)]
    mine = lane // NV == row % 8
    spread_out = [
        jnp.where(mine, jnp.where(row < 8, jnp.broadcast_to(lo, (NV, 128)), jnp.broadcast_to(hi, (NV, 128))), 0.0)
        for lo, hi in ((total[0], total[1]), (total[2], total[3]))
    ]
    spread_out = jnp.concatenate(spread_out, axis=0)
    source, target = iota((128, 128), 0), iota((128, 128), 1)
    squares = exact(spread_out, ones_where((source % NV == target % NV) & (target // NV % 2 == 0) & (target < 48)))
    turned = exact(ones_where(lane % NV == row), spread_out, ((1,), (1,)))
    fv, mixed = squares[0:NV, 0:NV], squares[NV:32, 0:NV]
    vf, mixed_t = turned[:, 0:NV], turned[:, NV:32]
    r, c = iota((NV, NV), 0), iota((NV, NV), 1)
    ff = jnp.where(c >= r, mixed, mixed_t)
    own = jnp.broadcast_to(total[4], (NV, 128))[:, 0:NV]
    vv = jnp.where(c < r, mixed, jnp.where(c > r, mixed_t, own))
    proj_ref[...] = vf
    gram = ff + exact(fv, exact(vv, vf) - 2.0 * vf)
    unit = ones_where(row + 16 == lane)
    a = jnp.pad(gram, ((0, 0), (0, 112))) + unit + jnp.where(lane >= 32, squares[0:NV], 0.0)
    columns = [jnp.broadcast_to(a[:, j : j + 1], (NV, 128)) for j in range(NV)]
    copies = []
    for k in range(0, NV, 2):
        col0, col1 = columns[k : k + 2]
        if k < NV - 2:
            at0, at1 = ({j: jnp.broadcast_to(m[j : j + 1], (NV, 128)) for j in range(k, NV)} for m in (col0, col1))
            p, q, t = at0[k], at1[k], at1[k + 1]
            scale = jnp.where(row > k + 1, 1.0 / (p * t - q * q), 0.0)
            step0, step1 = (col0 * t - col1 * q) * scale, (col1 * p - col0 * q) * scale
            row0, row1 = (jnp.broadcast_to(a[k + j : k + j + 1], (NV, 128)) for j in (0, 1))
            for j in range(k + 2, NV):
                columns[j] = columns[j] - step0 * at0[j] - step1 * at1[j]
            a = a - step0 * row0 - step1 * row1
    high, low = rows_done(a, r_ref)
    for x in range(NX):
        got = spread(xf_ref, xe_ref, xv_ref, high, low, x)
        for h in range(2):
            stage[:, x, 8 * h : 8 * h + 8, :] = got[:, NZ * h : NZ * h + NZ].reshape(NV, 8, NZ)
        if x % 1 == 1-1:
            at = (slice(None), pl.ds(x - 1 + 1, 1))
            copies.append(pltpu.make_async_copy(stage.at[at], new_ref.at[at], sems.at[x // 1]))
            copies[-1].start()
    for copy in copies:
        copy.wait()


def rows_done(a, r_ref):
    row, lane = iota((NV, 128), 0), iota((NV, 128), 1)
    above = pltpu.roll(a, 1, 0)
    before, pivot = (jnp.sum(jnp.where(lane == row - 1, m, 0.0), axis=1, keepdims=True) for m in (a, above))
    odd = row % 2 == 1
    a = a - jnp.where(odd, before / jnp.where(odd[:, 0:1], pivot, 1.0), 0.0) * above
    pivots = jnp.sum(jnp.where(row == lane, a, 0.0), axis=1, keepdims=True)
    a = a / jnp.sqrt(pivots)
    r_ref[...] = jnp.where(lane >= row, a, 0.0)[:, 0:NV]
    w = jnp.where(lane < 32, a, -a)
    w = jnp.broadcast_to(w[:, None, :], (NV, 8, 128)).reshape(128, 128)
    source, target = iota((128, 256), 0), iota((128, 256), 1)
    widen = jnp.where(source - 16 == target // 8, 1.0, 0.0).astype(BF16)
    keep = iota((128, 256), 0) % 8 == iota((128, 256), 1) % 8
    return [
        jnp.where(keep, jnp.dot(part, widen, preferred_element_type=F32), 0.0).astype(BF16) for part in two_parts(w)
    ]


def spread(xf_ref, xe_ref, xv_ref, high, low, x):
    if x in (0, NX - 1):
        f_ref, at = xe_ref, x // (NX - 1)
    else:
        f_ref, at = xf_ref, x - 1
    f_cols, v_cols = slice(256 * at, 256 * at + 256), slice(256 * x, 256 * x + 256)
    fh, fl = f_ref[0:128, f_cols], f_ref[128:256, f_cols]
    vh, vl = xv_ref[0:128, v_cols], xv_ref[128:256, v_cols]
    left = jnp.concatenate([high, high, low], axis=1)
    return jnp.dot(left, jnp.concatenate([fh, vh, fl, vl, fh, vh], axis=0), preferred_element_type=F32)


def finish(parts, xf, xe, xv):
    return pl.pallas_call(
        finish_kernel,
        out_shape=(
            jax.ShapeDtypeStruct((NV, NX, NY, NZ), F32),
            jax.ShapeDtypeStruct((NV, NV), F32),
            jax.ShapeDtypeStruct((NV, NV), F32),
        ),
        in_specs=[VMEM] * 4,
        out_specs=(pl.BlockSpec(memory_space=pl.ANY), VMEM, VMEM),
        scratch_shapes=[pltpu.VMEM((NV, NX, NY, NZ), F32), pltpu.SemaphoreType.DMA((NX,))],
        compiler_params=pltpu.CompilerParams(vmem_limit_bytes=16 << 20),
        cost_estimate=pl.CostEstimate(flops=1 << 29, bytes_accessed=3 << 20, transcendentals=0),
        name="finish",
    )(parts, xf, xe, xv)


def sent_to_all(x, axes):
    peers = lax.axis_size(axes)
    return lax.all_to_all(jnp.broadcast_to(x[None], (peers, *x.shape)), axes, 0, 0, tiled=True)


def shards(krylov_basis_block, companion, region, inv_density, stiffness, damping):
    core = lax.axis_index("slab_3").astype(jnp.int32).reshape(1)
    count = lax.axis_size(SLAB)
    *own, fields = pack(core, inv_density, stiffness, damping, krylov_basis_block, region, companion)
    pairs = [(i, i ^ 1) for i in range(count)]
    across = [(i, i + 1 if i % 2 else i - 1) for i in range(1, count - 1)]
    got0 = lax.ppermute(own[0], SLAB, across)
    got1 = lax.ppermute(own[1], SLAB, pairs)
    xf, xv, edges, tiles = main(krylov_basis_block, fields, companion)
    xe, packed, xf = edge(core, edges, tiles, xv, own, (got0, got1), xf)
    near = sent_to_all(packed.reshape(1, 640), ("slab_1", "slab_2")).sum(axis=0)
    far = sent_to_all(near.reshape(1, 640), ("slab_0", "slab_3"))
    new_block, projection, rfactor = finish(far.reshape(-1, 128), xf, xe, xv)
    return new_block, projection, rfactor


def solution(mesh):
    torus = Mesh(mesh.devices.reshape(8, 4, 8, 2), SLAB)
    placed = (
        P(None, SLAB, None, None),
        P(None, SLAB, None, None),
        P(SLAB, None, None),
        P(),
        P(),
        P(),
    )
    return jax.shard_map(
        shards,
        mesh=torus,
        in_specs=placed,
        out_specs=(P(None, SLAB, None, None), P(), P()),
        check_vma=False,
    )
```

time: 53.6 us -> 52.7 us (0.983)
  blocking collectives: 35.6 us -> 34.9 us
    all_to_all x2, blocking collectives: 35.6 us -> 34.9 us  [sent_to_all(): lax.all_to_all(jnp.broadcast_to(x[None], (peers, *x.shape)), axes, 0, 0,...]
    pallas_call x1, Pallas kernels: 3.6 us -> 2.98 us  [finish(): pl.pallas_call(finish_kernel, out_shape=(jax.ShapeDtypeStruct((NV, NX, NY...]
  transfers between devices with their start and end apart: 2 -> 2, of which waited for: 0 -> 0; matrix products, arithmetic and copies ran while one was open for 0% -> 0% of each run, Pallas kernels for 3% -> 4%
where the time goes in v4:
time: 52.7 us; the launch traced here: 52.4 us
  blocking collectives  34.9 us (66%)
  starting transfers between devices  9.42 us (18%)
  Pallas kernels  7.16 us (14%)
  between operations  0.73 us (1%)
    all_to_all x2, blocking collectives, sent_to_all(): lax.all_to_all(jnp.broadcast_to(x[None], (peers, *x.shape)), axes, 0, 0,...  34.9 us
    ppermute x1, starting transfers between devices, shards(): got1 = lax.ppermute(own[1], SLAB, pairs)  4.83 us
    ppermute x1, starting transfers between devices, shards(): got0 = lax.ppermute(own[0], SLAB, across)  4.58 us
    pallas_call x1, Pallas kernels, finish(): pl.pallas_call(finish_kernel, out_shape=(jax.ShapeDtypeStruct((NV, NX, NY...  2.98 us
    pallas_call x1, Pallas kernels, main(): pl.pallas_call(main_kernel, out_shape=(jax.ShapeDtypeStruct((256, 1536),...  2.08 us
    pallas_call x1, Pallas kernels, pack(): pl.pallas_call(pack_kernel, out_shape=(plane, plane, jax.ShapeDtypeStruct...  1.2 us
  transfers between devices with their start and end apart: 2, of which 0 were waited for; matrix products, arithmetic and copies ran while one was open for 0% of the time, Pallas kernels for 4%

profile of v4, /device:TPU:1, one launch (start us, length us, event | category | flops | bytes accessed | tf_op | source)
XLA Modules:
  0.0 52.4 jit_solution(1356976636906490566)
XLA Ops:
  0.6 0.0 copy-start
  0.6 0.0 copy-start.1
  0.7 1.2 %pack.1 = (f32[17,16,128]{2,1,0:T(8,128)S(1)}, f32[17,16,128]{2,1,0:T(8,128)S(1)}, f32[3,8,16,128]{3,2,1,0:T(8,128)S(1)}) custom-call(s32[1]{0:T(128)} %bitcast.core, f32[8]{0:T(128)} %dens_ref.1, f32[8]{0:T(128)} %stiff_ref.1, f32[8]{0:T(128)} %damp_ref.1, f32[16,8,16,128]{3,2,1,0:T(8,128)} %v_ref.3, s32[8,16,128]{2,1,0:T(8,128)} %region_ref.1, ...), custom_call_target="tpu_custom_call" | custom-call | flops 262144 | bytes 524288 | tf_op jit(solution)/shard_map/pack/pallas_call | solution.py:59
  1.9 4.6 %collective-permute-start = (f32[17,16,128]{2,1,0:T(8,128)S(1)}, f32[17,16,128]{2,1,0:T(8,128)S(1)}, u32[]{:S(2)}, u32[]{:S(2)}) collective-permute-start(f32[17,16,128]{2,1,0:T(8,128)S(1)} %get-tuple-element.17.own0), channel_id=1, source_target_pairs={{1,2},{2,1},{3,4},{4,3},{5,6},{6,5},{7,8},{8,7},{9,10},{10,9},{11,... | collective-permute-start | bytes 417800 | tf_op jit(solution)/shard_map/ppermute | solution.py:348
  6.5 4.8 %collective-permute-start.1 = (f32[17,16,128]{2,1,0:T(8,128)S(1)}, f32[17,16,128]{2,1,0:T(8,128)S(1)}, u32[]{:S(2)}, u32[]{:S(2)}) collective-permute-start(f32[17,16,128]{2,1,0:T(8,128)S(1)} %get-tuple-element.18.own1), channel_id=1, source_target_pairs={{0,1},{1,0},{2,3},{3,2},{4,5},{5,4},{6,7},{7,6},{8,9},{9,8},{10,11... | collective-permute-start | bytes 417800 | tf_op jit(solution)/shard_map/ppermute | solution.py:349
  11.3 0.0 copy-done
  11.3 0.0 copy-done.1
  11.3 2.1 %main.1 = (bf16[256,1536]{1,0:T(8,128)(2,1)S(1)}, bf16[256,2048]{1,0:T(8,128)(2,1)S(1)}, f32[2,16,16,128]{3,2,1,0:T(8,128)S(1)}, f32[48,128]{1,0:T(8,128)S(1)}) custom-call(f32[16,8,16,128]{3,2,1,0:T(8,128)S(1)} %copy-done, f32[3,8,16,128]{3,2,1,0:T(8,128)S(1)} %get-tuple-element.13.fields, f32[16,8,16,128]{3,2,1,0:T(8,128)S(1)} %copy-done.1), custom_call_target="tpu_custom_call" | custom-call | flops 268435456 | bytes 5242880 | tf_op jit(solution)/shard_map/main/pallas_call | solution.py:174
  13.4 0.0 collective-permute-done.got0
  13.4 0.0 collective-permute-done.1.got1
  13.5 0.9 %edge.1 = (bf16[256,512]{1,0:T(8,128)(2,1)S(1)}, f32[5,128]{1,0:T(8,128)S(1)}, bf16[256,1536]{1,0:T(8,128)(2,1)S(1)}) custom-call(s32[1]{0:T(128)} %bitcast.core, f32[2,16,16,128]{3,2,1,0:T(8,128)S(1)} %get-tuple-element.14.edge_ref, f32[48,128]{1,0:T(8,128)S(1)} %get-tuple-element.15.tiles_ref, ...), custom_call_target="tpu_custom_call", output_to_operand_aliasing={{2}: (8, {})} | custom-call | flops 134217728 | bytes 2097152 | tf_op jit(solution)/shard_map/edge/pallas_call | solution.py:225
  14.4 15.6 %all_to_all.10 = f32[32,1,640]{2,1,0:T(1,128)S(1)} all-to-all(f32[32,1,640]{2,1,0:T(1,128)S(1)} %broadcast_in_dim.14), channel_id=1, replica_groups=mesh['slab_0'=8,'slab_1'=4,'slab_2'=8,'slab_3'=2] {'slab_1','slab_2'}, dimensions={0} | all-to-all | bytes 163840 | tf_op jit(solution)/shard_map/all_to_all | solution.py:339
  30.0 0.1 reduce_sum.9
  30.1 19.3 %all_to_all.11 = f32[16,1,640]{2,1,0:T(1,128)S(1)} all-to-all(f32[16,1,640]{2,1,0:T(1,128)S(1)} %broadcast_in_dim.15), channel_id=1, replica_groups=mesh['slab_0'=8,'slab_1'=4,'slab_2'=8,'slab_3'=2] {'slab_0','slab_3'}, dimensions={0} | all-to-all | bytes 81920 | tf_op jit(solution)/shard_map/all_to_all | solution.py:339
  49.4 3.0 %finish.1 = (f32[16,8,16,128]{3,2,1,0:T(8,128)}, f32[16,16]{1,0:T(8,128)}, f32[16,16]{1,0:T(8,128)}) custom-call(f32[80,128]{1,0:T(8,128)S(1)} %bitcast.3, bf16[256,1536]{1,0:T(8,128)(2,1)S(1)} %get-tuple-element.21.xf_ref, bf16[256,512]{1,0:T(8,128)(2,1)S(1)} %get-tuple-element.22.xe_ref, bf16[256,2048]{1,0:T(8,128)(2,1)S(1)} %get-tuple-element.16.xv_ref), custom_call_target="tpu_custom_call" | custom-call | flops 536870912 | bytes 3145728 | tf_op jit(solution)/shard_map/finish/pallas_call | solution.py:321
  (2 shorter events, 0.1 us)
Async XLA Ops:
  0.6 10.7 %copy-start = (f32[16,8,16,128]{3,2,1,0:T(8,128)S(1)}, f32[16,8,16,128]{3,2,1,0:T(8,128)}, u32[]{:S(2)}) copy-start(f32[16,8,16,128]{3,2,1,0:T(8,128)} %v_ref.3) | copy-start | bytes 3145732
  0.6 10.7 %copy-start.1 = (f32[16,8,16,128]{3,2,1,0:T(8,128)S(1)}, f32[16,8,16,128]{3,2,1,0:T(8,128)}, u32[]{:S(2)}) copy-start(f32[16,8,16,128]{3,2,1,0:T(8,128)} %comp_ref.3) | copy-start | bytes 3145732
  1.9 11.6 %collective-permute-start = (f32[17,16,128]{2,1,0:T(8,128)S(1)}, f32[17,16,128]{2,1,0:T(8,128)S(1)}, u32[]{:S(2)}, u32[]{:S(2)}) collective-permute-start(f32[17,16,128]{2,1,0:T(8,128)S(1)} %get-tuple-element.17.own0), channel_id=1, source_target_pairs={{1,2},{2,1},{3,4},{4,3},{5,6},{6,5},{7,8},{8,7},{9,10},{10,9},{11,... | collective-permute-start | bytes 417800 | tf_op jit(solution)/shard_map/ppermute | solution.py:348
  6.5 7.0 %collective-permute-start.1 = (f32[17,16,128]{2,1,0:T(8,128)S(1)}, f32[17,16,128]{2,1,0:T(8,128)S(1)}, u32[]{:S(2)}, u32[]{:S(2)}) collective-permute-start(f32[17,16,128]{2,1,0:T(8,128)S(1)} %get-tuple-element.18.own1), channel_id=1, source_target_pairs={{0,1},{1,0},{2,3},{3,2},{4,5},{5,4},{6,7},{7,6},{8,9},{9,8},{10,11... | collective-permute-start | bytes 417800 | tf_op jit(solution)/shard_map/ppermute | solution.py:349

commit v5 on v4

--- a/solution.py
+++ b/solution.py
@@ -28,7 +28,7 @@
     return [pltpu.with_memory_space_constraint(a, pltpu.HBM) for a in arrays]
 
 
-def pack_kernel(core, dens_ref, stiff_ref, damp_ref, v_ref, region_ref, comp_ref, out0, out1, fields, tables, regions, sems):
+def pack_kernel(core, dens_ref, stiff_ref, damp_ref, v_ref, region_ref, out0, out1, fields, tables, regions, sems):
     outs = (out0, out1)
     at = ((NX - 1) * core[0], (NX - 1) * (1 - core[0]))
     whole = pltpu.make_async_copy(region_ref, regions, sems.at[0])
@@ -54,12 +54,12 @@
         copy.wait()
 
 
-def pack(core, dens, stiff, dampt, basis, region, companion):
+def pack(core, dens, stiff, dampt, basis, region):
     plane = jax.ShapeDtypeStruct((NV + 1, NY, NZ), F32)
     return pl.pallas_call(
         pack_kernel,
         out_shape=(plane, plane, jax.ShapeDtypeStruct((3, NX, NY, NZ), F32)),
-        in_specs=[SMEM] + [HBM] * 6,
+        in_specs=[SMEM] + [HBM] * 5,
         out_specs=(VMEM,) * 3,
         scratch_shapes=[
             pltpu.SMEM((3, NR), F32),
@@ -69,7 +69,7 @@
         compiler_params=pltpu.CompilerParams(vmem_limit_bytes=4 << 20),
         cost_estimate=pl.CostEstimate(flops=1 << 18, bytes_accessed=1 << 19, transcendentals=0),
         name="pack",
-    )(core, *in_hbm(dens, stiff, dampt, basis, region, companion))
+    )(core, *in_hbm(dens, stiff, dampt, basis, region))
 
 
 def exact(left, right, dims=((1,), (0,))):
@@ -100,6 +100,29 @@
 
 def times_turned(left, right):
     return lax.dot_general(left, right, (((1,), (1,)), ((), ())), preferred_element_type=F32)
+
+
+def products(high, low, right_high, right_low):
+    left = jnp.concatenate([high, high, low], axis=1)
+    right = jnp.concatenate([right_high, right_low, right_high], axis=1)
+    return times_turned(left, right)
+
+
+def hold_kernel(fields, basis, companion, out):
+    pass
+
+
+def hold(fields, basis, companion):
+    anywhere = pl.BlockSpec(memory_space=pl.ANY)
+    return pl.pallas_call(
+        hold_kernel,
+        out_shape=jax.ShapeDtypeStruct(fields.shape, fields.dtype),
+        in_specs=[anywhere, HBM, HBM],
+        out_specs=anywhere,
+        input_output_aliases={0: 0},
+        compiler_params=pltpu.CompilerParams(vmem_limit_bytes=1 << 20),
+        name="hold",
+    )(fields, *in_hbm(basis, companion))
 
 
 def main_kernel(v_ref, fields, comp_ref, xf_ref, xv_ref, edge_ref, tiles_ref):
@@ -203,12 +226,9 @@
     fh, fl = xe_ref[0:128], xe_ref[128:256]
     ends = (slice(0, 2 * NZ), slice(14 * NZ, 16 * NZ))
     vh, vl = (jnp.concatenate([xv_ref[k : k + 128, e] for e in ends], axis=1) for k in (0, 128))
-    high, low = jnp.concatenate([fh, vh], axis=0), jnp.concatenate([fl, vl], axis=0)
-    sums = folded(
-        times_turned(jnp.concatenate([fh, fh, fl], axis=1), jnp.concatenate([high, low, high], axis=1))
-    )
-    ff = tiled(sums[:, 0:128]) + tiles_ref[0:NV]
-    fv = tiled(sums[:, 128:256]) + tiles_ref[NV:32]
+    sums = folded(products(fh, fl, jnp.concatenate([fh, vh], axis=0), jnp.concatenate([fl, vl], axis=0)))
+    over = tiled(jnp.concatenate([sums[:, 0:128], sums[:, 128:256]], axis=0)) + tiles_ref[0:32]
+    ff, fv = over[0:NV], over[NV:32]
     vv = tiles_ref[32:48]
     row, lane = iota((NV, 128), 0), iota((NV, 128), 1)
     sums = []
@@ -236,6 +256,13 @@
         cost_estimate=pl.CostEstimate(flops=1 << 27, bytes_accessed=2 << 20, transcendentals=0),
         name="edge",
     )(core, edges, tiles, xv, *own, *got, xf)
+
+
+def summed(left, right):
+    terms = [left[:, k : k + 1] * right[k : k + 1] for k in range(NV)]
+    while len(terms) > 1:
+        terms = [a + b for a, b in zip(terms[::2], terms[1::2])]
+    return terms[0]
 
 
 def finish_kernel(parts_ref, xf_ref, xe_ref, xv_ref, new_ref, proj_ref, r_ref, stage, sems):
@@ -257,7 +284,7 @@
     own = jnp.broadcast_to(total[4], (NV, 128))[:, 0:NV]
     vv = jnp.where(c < r, mixed, jnp.where(c > r, mixed_t, own))
     proj_ref[...] = vf
-    gram = ff + exact(fv, exact(vv, vf) - 2.0 * vf)
+    gram = ff + summed(fv, summed(vv, vf) - 2.0 * vf)
     unit = ones_where(row + 16 == lane)
     a = jnp.pad(gram, ((0, 0), (0, 112))) + unit + jnp.where(lane >= 32, squares[0:NV], 0.0)
     columns = [jnp.broadcast_to(a[:, j : j + 1], (NV, 128)) for j in range(NV)]
@@ -342,7 +369,8 @@
 def shards(krylov_basis_block, companion, region, inv_density, stiffness, damping):
     core = lax.axis_index("slab_3").astype(jnp.int32).reshape(1)
     count = lax.axis_size(SLAB)
-    *own, fields = pack(core, inv_density, stiffness, damping, krylov_basis_block, region, companion)
+    *own, fields = pack(core, inv_density, stiffness, damping, krylov_basis_block, region)
+    own[0] = hold(own[0], krylov_basis_block, companion)
     pairs = [(i, i ^ 1) for i in range(count)]
     across = [(i, i + 1 if i % 2 else i - 1) for i in range(1, count - 1)]
     got0 = lax.ppermute(own[0], SLAB, across)

time: 52.7 us -> 52.4 us (level)
  no operation moved by 1% of the time
where the time goes in v5:
time: 52.4 us; the launch traced here: 52.2 us
  blocking collectives  34.9 us (67%)
  starting transfers between devices  9.55 us (18%)
  Pallas kernels  6.77 us (13%)
  between operations  0.74 us (1%)
    all_to_all x2, blocking collectives, sent_to_all(): lax.all_to_all(jnp.broadcast_to(x[None], (peers, *x.shape)), axes, 0, 0,...  34.9 us
    ppermute x1, starting transfers between devices, shards(): got1 = lax.ppermute(own[1], SLAB, pairs)  4.83 us
    ppermute x1, starting transfers between devices, shards(): got0 = lax.ppermute(own[0], SLAB, across)  4.71 us
    pallas_call x1, Pallas kernels, finish(): pl.pallas_call(finish_kernel, out_shape=(jax.ShapeDtypeStruct((NV, NX, NY...  2.85 us
    pallas_call x1, Pallas kernels, main(): pl.pallas_call(main_kernel, out_shape=(jax.ShapeDtypeStruct((256, 1536),...  2.08 us
    pallas_call x1, Pallas kernels, pack(): pl.pallas_call(pack_kernel, out_shape=(plane, plane, jax.ShapeDtypeStruct...  1.06 us
  transfers between devices with their start and end apart: 2, of which 0 were waited for; matrix products, arithmetic and copies ran while one was open for 0% of the time, Pallas kernels for 4%

profile of v5, /device:TPU:1, one launch (start us, length us, event | category | flops | bytes accessed | tf_op | source)
XLA Modules:
  0.0 52.2 jit_solution(11257397032993784032)
XLA Ops:
  0.6 1.1 %pack.1 = (f32[17,16,128]{2,1,0:T(8,128)S(1)}, f32[17,16,128]{2,1,0:T(8,128)S(1)}, f32[3,8,16,128]{3,2,1,0:T(8,128)S(1)}) custom-call(s32[1]{0:T(128)} %bitcast.core, f32[8]{0:T(128)} %dens_ref.1, f32[8]{0:T(128)} %stiff_ref.1, f32[8]{0:T(128)} %damp_ref.1, f32[16,8,16,128]{3,2,1,0:T(8,128)} %basis.1, s32[8,16,128]{2,1,0:T(8,128)} %region_ref.1), custom_call_target="tpu_custom_call" | custom-call | flops 262144 | bytes 524288 | tf_op jit(solution)/shard_map/pack/pallas_call | solution.py:59
  1.7 0.0 copy-start
  1.7 0.0 copy-start.1
  1.7 4.7 %collective-permute-start = (f32[17,16,128]{2,1,0:T(8,128)S(1)}, f32[17,16,128]{2,1,0:T(8,128)S(1)}, u32[]{:S(2)}, u32[]{:S(2)}) collective-permute-start(f32[17,16,128]{2,1,0:T(8,128)S(1)} %hold.1.own0), channel_id=1, source_target_pairs={{1,2},{2,1},{3,4},{4,3},{5,6},{6,5},{7,8},{8,7},{9,10},{10,9},{11,... | collective-permute-start | bytes 417800 | tf_op jit(solution)/shard_map/ppermute | solution.py:376
  6.5 4.8 %collective-permute-start.1 = (f32[17,16,128]{2,1,0:T(8,128)S(1)}, f32[17,16,128]{2,1,0:T(8,128)S(1)}, u32[]{:S(2)}, u32[]{:S(2)}) collective-permute-start(f32[17,16,128]{2,1,0:T(8,128)S(1)} %get-tuple-element.18.own1), channel_id=1, source_target_pairs={{0,1},{1,0},{2,3},{3,2},{4,5},{5,4},{6,7},{7,6},{8,9},{9,8},{10,11... | collective-permute-start | bytes 417800 | tf_op jit(solution)/shard_map/ppermute | solution.py:377
  11.3 0.0 copy-done
  11.3 0.0 copy-done.1
  11.3 2.1 %main.1 = (bf16[256,1536]{1,0:T(8,128)(2,1)S(1)}, bf16[256,2048]{1,0:T(8,128)(2,1)S(1)}, f32[2,16,16,128]{3,2,1,0:T(8,128)S(1)}, f32[48,128]{1,0:T(8,128)S(1)}) custom-call(f32[16,8,16,128]{3,2,1,0:T(8,128)S(1)} %copy-done, f32[3,8,16,128]{3,2,1,0:T(8,128)S(1)} %get-tuple-element.13.fields, f32[16,8,16,128]{3,2,1,0:T(8,128)S(1)} %copy-done.1), custom_call_target="tpu_custom_call" | custom-call | flops 268435456 | bytes 5242880 | tf_op jit(solution)/shard_map/main/pallas_call | solution.py:197
  13.4 0.0 collective-permute-done.got0
  13.4 0.0 collective-permute-done.1.got1
  13.5 0.8 %edge.1 = (bf16[256,512]{1,0:T(8,128)(2,1)S(1)}, f32[5,128]{1,0:T(8,128)S(1)}, bf16[256,1536]{1,0:T(8,128)(2,1)S(1)}) custom-call(s32[1]{0:T(128)} %bitcast.core, f32[2,16,16,128]{3,2,1,0:T(8,128)S(1)} %get-tuple-element.14.edge_ref, f32[48,128]{1,0:T(8,128)S(1)} %get-tuple-element.15.tiles_ref, ...), custom_call_target="tpu_custom_call", output_to_operand_aliasing={{2}: (8, {})} | custom-call | flops 134217728 | bytes 2097152 | tf_op jit(solution)/shard_map/edge/pallas_call | solution.py:245
  14.3 15.6 %all_to_all.10 = f32[32,1,640]{2,1,0:T(1,128)S(1)} all-to-all(f32[32,1,640]{2,1,0:T(1,128)S(1)} %broadcast_in_dim.14), channel_id=1, replica_groups=mesh['slab_0'=8,'slab_1'=4,'slab_2'=8,'slab_3'=2] {'slab_1','slab_2'}, dimensions={0} | all-to-all | bytes 163840 | tf_op jit(solution)/shard_map/all_to_all | solution.py:366
  29.9 0.1 reduce_sum.9
  30.0 19.3 %all_to_all.11 = f32[16,1,640]{2,1,0:T(1,128)S(1)} all-to-all(f32[16,1,640]{2,1,0:T(1,128)S(1)} %broadcast_in_dim.15), channel_id=1, replica_groups=mesh['slab_0'=8,'slab_1'=4,'slab_2'=8,'slab_3'=2] {'slab_0','slab_3'}, dimensions={0} | all-to-all | bytes 81920 | tf_op jit(solution)/shard_map/all_to_all | solution.py:366
  49.3 2.9 %finish.1 = (f32[16,8,16,128]{3,2,1,0:T(8,128)}, f32[16,16]{1,0:T(8,128)}, f32[16,16]{1,0:T(8,128)}) custom-call(f32[80,128]{1,0:T(8,128)S(1)} %bitcast.3, bf16[256,1536]{1,0:T(8,128)(2,1)S(1)} %get-tuple-element.21.xf_ref, bf16[256,512]{1,0:T(8,128)(2,1)S(1)} %get-tuple-element.22.xe_ref, bf16[256,2048]{1,0:T(8,128)(2,1)S(1)} %get-tuple-element.16.xv_ref), custom_call_target="tpu_custom_call" | custom-call | flops 536870912 | bytes 3145728 | tf_op jit(solution)/shard_map/finish/pallas_call | solution.py:348
  (3 shorter events, 0.1 us)
Async XLA Ops:
  1.7 9.6 %copy-start = (f32[16,8,16,128]{3,2,1,0:T(8,128)S(1)}, f32[16,8,16,128]{3,2,1,0:T(8,128)}, u32[]{:S(2)}) copy-start(f32[16,8,16,128]{3,2,1,0:T(8,128)} %basis.1) | copy-start | bytes 3145732
  1.7 9.6 %copy-start.1 = (f32[16,8,16,128]{3,2,1,0:T(8,128)S(1)}, f32[16,8,16,128]{3,2,1,0:T(8,128)}, u32[]{:S(2)}) copy-start(f32[16,8,16,128]{3,2,1,0:T(8,128)} %companion.1) | copy-start | bytes 3145732
  1.7 11.7 %collective-permute-start = (f32[17,16,128]{2,1,0:T(8,128)S(1)}, f32[17,16,128]{2,1,0:T(8,128)S(1)}, u32[]{:S(2)}, u32[]{:S(2)}) collective-permute-start(f32[17,16,128]{2,1,0:T(8,128)S(1)} %hold.1.own0), channel_id=1, source_target_pairs={{1,2},{2,1},{3,4},{4,3},{5,6},{6,5},{7,8},{8,7},{9,10},{10,9},{11,... | collective-permute-start | bytes 417800 | tf_op jit(solution)/shard_map/ppermute | solution.py:376
  6.5 7.0 %collective-permute-start.1 = (f32[17,16,128]{2,1,0:T(8,128)S(1)}, f32[17,16,128]{2,1,0:T(8,128)S(1)}, u32[]{:S(2)}, u32[]{:S(2)}) collective-permute-start(f32[17,16,128]{2,1,0:T(8,128)S(1)} %get-tuple-element.18.own1), channel_id=1, source_target_pairs={{0,1},{1,0},{2,3},{3,2},{4,5},{5,4},{6,7},{7,6},{8,9},{9,8},{10,11... | collective-permute-start | bytes 417800 | tf_op jit(solution)/shard_map/ppermute | solution.py:377

commit v6 on v5

--- a/solution.py
+++ b/solution.py
@@ -72,16 +72,25 @@
     )(core, *in_hbm(dens, stiff, dampt, basis, region))
 
 
-def exact(left, right, dims=((1,), (0,))):
-    return lax.dot_general(left, right, (dims, ((), ())), precision=lax.Precision.HIGHEST, preferred_element_type=F32)
-
-
 def iota(shape, axis):
     return lax.broadcasted_iota(jnp.int32, shape, axis)
 
 
 def ones_where(condition):
     return jnp.where(condition, 1.0, 0.0).astype(F32)
+
+
+def picked(values, chosen, dims=((1,), (0,)), values_first=True):
+    first, rest = values.astype(BF16), values
+    parts = [first]
+    for _ in range(2):
+        rest = rest - parts[-1].astype(F32)
+        parts.append(rest.astype(BF16))
+    ones = jnp.where(chosen, 1.0, 0.0).astype(BF16)
+    values_dim, ones_dim = (dims[0][0], dims[1][0]) if values_first else (dims[1][0], dims[0][0])
+    values, ones = jnp.concatenate(parts, axis=values_dim), jnp.concatenate([ones] * 3, axis=ones_dim)
+    left, right = (values, ones) if values_first else (ones, values)
+    return lax.dot_general(left, right, (dims, ((), ())), preferred_element_type=F32)
 
 
 def folded(full):
@@ -91,7 +100,7 @@
 
 
 def tiled(half):
-    return exact(half, ones_where(iota((128, 128), 0) // 8 == iota((128, 128), 1) % NV))
+    return picked(half, iota((128, 128), 0) // 8 == iota((128, 128), 1) % NV)
 
 
 def beside(square):
@@ -182,11 +191,10 @@
         for right, end_right in ((high, end_high), (low, end_low))
     )
     both = same + mixed
-    square = exact(mixed, ones_where(iota((256, 128), 0) // 8 == iota((256, 128), 1)))
     group, lane = iota((32, 128), 0), iota((32, 128), 1)
     over_f, over_v = (
         tiled(both[:, 128 * k : 128 * k + 128])
-        + exact(square, ones_where(group - NV * k == lane % NV), ((0,), (0,)))[0:32]
+        + jnp.sum(picked(mixed, group - NV * k == lane % NV, ((0,), (0,))).reshape(32, 8, 128), axis=1)
         for k in (0, 1)
     )
     tiles_ref[0:NV] = over_f[0:NV]
@@ -275,8 +283,8 @@
     ]
     spread_out = jnp.concatenate(spread_out, axis=0)
     source, target = iota((128, 128), 0), iota((128, 128), 1)
-    squares = exact(spread_out, ones_where((source % NV == target % NV) & (target // NV % 2 == 0) & (target < 48)))
-    turned = exact(ones_where(lane % NV == row), spread_out, ((1,), (1,)))
+    squares = picked(spread_out, (source % NV == target % NV) & (target // NV % 2 == 0) & (target < 48))
+    turned = picked(spread_out, lane % NV == row, ((1,), (1,)), values_first=False)
     fv, mixed = squares[0:NV, 0:NV], squares[NV:32, 0:NV]
     vf, mixed_t = turned[:, 0:NV], turned[:, NV:32]
     r, c = iota((NV, NV), 0), iota((NV, NV), 1)

time: 52.4 us -> 52.2 us (level)
  no operation moved by 1% of the time
where the time goes in v6:
time: 52.2 us; the launch traced here: 52 us
  blocking collectives  35.1 us (67%)
  starting transfers between devices  9.55 us (18%)
  Pallas kernels  6.42 us (12%)
  between operations  0.74 us (1%)
    all_to_all x2, blocking collectives, sent_to_all(): lax.all_to_all(jnp.broadcast_to(x[None], (peers, *x.shape)), axes, 0, 0,...  35.1 us
    ppermute x1, starting transfers between devices, shards(): got1 = lax.ppermute(own[1], SLAB, pairs)  4.83 us
    ppermute x1, starting transfers between devices, shards(): got0 = lax.ppermute(own[0], SLAB, across)  4.71 us
    pallas_call x1, Pallas kernels, finish(): pl.pallas_call(finish_kernel, out_shape=(jax.ShapeDtypeStruct((NV, NX, NY...  2.85 us
    pallas_call x1, Pallas kernels, main(): pl.pallas_call(main_kernel, out_shape=(jax.ShapeDtypeStruct((256, 1536),...  1.88 us
    pallas_call x1, Pallas kernels, pack(): pl.pallas_call(pack_kernel, out_shape=(plane, plane, jax.ShapeDtypeStruct...  1.06 us
  transfers between devices with their start and end apart: 2, of which 0 were waited for; matrix products, arithmetic and copies ran while one was open for 0% of the time, Pallas kernels for 4%

profile of v6, /device:TPU:1, one launch (start us, length us, event | category | flops | bytes accessed | tf_op | source)
XLA Modules:
  0.0 52.0 jit_solution(3696355234272295822)
XLA Ops:
  0.6 1.1 %pack.1 = (f32[17,16,128]{2,1,0:T(8,128)S(1)}, f32[17,16,128]{2,1,0:T(8,128)S(1)}, f32[3,8,16,128]{3,2,1,0:T(8,128)S(1)}) custom-call(s32[1]{0:T(128)} %bitcast.core, f32[8]{0:T(128)} %dens_ref.1, f32[8]{0:T(128)} %stiff_ref.1, f32[8]{0:T(128)} %damp_ref.1, f32[16,8,16,128]{3,2,1,0:T(8,128)} %basis.1, s32[8,16,128]{2,1,0:T(8,128)} %region_ref.1), custom_call_target="tpu_custom_call" | custom-call | flops 262144 | bytes 524288 | tf_op jit(solution)/shard_map/pack/pallas_call | solution.py:59
  1.7 0.0 copy-start
  1.7 0.0 copy-start.1
  1.7 4.7 %collective-permute-start = (f32[17,16,128]{2,1,0:T(8,128)S(1)}, f32[17,16,128]{2,1,0:T(8,128)S(1)}, u32[]{:S(2)}, u32[]{:S(2)}) collective-permute-start(f32[17,16,128]{2,1,0:T(8,128)S(1)} %hold.1.own0), channel_id=1, source_target_pairs={{1,2},{2,1},{3,4},{4,3},{5,6},{6,5},{7,8},{8,7},{9,10},{10,9},{11,... | collective-permute-start | bytes 417800 | tf_op jit(solution)/shard_map/ppermute | solution.py:384
  6.5 4.8 %collective-permute-start.1 = (f32[17,16,128]{2,1,0:T(8,128)S(1)}, f32[17,16,128]{2,1,0:T(8,128)S(1)}, u32[]{:S(2)}, u32[]{:S(2)}) collective-permute-start(f32[17,16,128]{2,1,0:T(8,128)S(1)} %get-tuple-element.18.own1), channel_id=1, source_target_pairs={{0,1},{1,0},{2,3},{3,2},{4,5},{5,4},{6,7},{7,6},{8,9},{9,8},{10,11... | collective-permute-start | bytes 417800 | tf_op jit(solution)/shard_map/ppermute | solution.py:385
  11.3 0.0 copy-done
  11.3 0.0 copy-done.1
  11.3 1.9 %main.1 = (bf16[256,1536]{1,0:T(8,128)(2,1)S(1)}, bf16[256,2048]{1,0:T(8,128)(2,1)S(1)}, f32[2,16,16,128]{3,2,1,0:T(8,128)S(1)}, f32[48,128]{1,0:T(8,128)S(1)}) custom-call(f32[16,8,16,128]{3,2,1,0:T(8,128)S(1)} %copy-done, f32[3,8,16,128]{3,2,1,0:T(8,128)S(1)} %get-tuple-element.13.fields, f32[16,8,16,128]{3,2,1,0:T(8,128)S(1)} %copy-done.1), custom_call_target="tpu_custom_call" | custom-call | flops 268435456 | bytes 5242880 | tf_op jit(solution)/shard_map/main/pallas_call | solution.py:205
  13.2 0.0 collective-permute-done.got0
  13.2 0.0 collective-permute-done.1.got1
  13.2 0.6 %edge.1 = (bf16[256,512]{1,0:T(8,128)(2,1)S(1)}, f32[5,128]{1,0:T(8,128)S(1)}, bf16[256,1536]{1,0:T(8,128)(2,1)S(1)}) custom-call(s32[1]{0:T(128)} %bitcast.core, f32[2,16,16,128]{3,2,1,0:T(8,128)S(1)} %get-tuple-element.14.edge_ref, f32[48,128]{1,0:T(8,128)S(1)} %get-tuple-element.15.tiles_ref, ...), custom_call_target="tpu_custom_call", output_to_operand_aliasing={{2}: (8, {})} | custom-call | flops 134217728 | bytes 2097152 | tf_op jit(solution)/shard_map/edge/pallas_call | solution.py:253
  13.9 15.8 %all_to_all.10 = f32[32,1,640]{2,1,0:T(1,128)S(1)} all-to-all(f32[32,1,640]{2,1,0:T(1,128)S(1)} %broadcast_in_dim.14), channel_id=1, replica_groups=mesh['slab_0'=8,'slab_1'=4,'slab_2'=8,'slab_3'=2] {'slab_1','slab_2'}, dimensions={0} | all-to-all | bytes 163840 | tf_op jit(solution)/shard_map/all_to_all | solution.py:374
  29.8 0.1 reduce_sum.9
  29.9 19.3 %all_to_all.11 = f32[16,1,640]{2,1,0:T(1,128)S(1)} all-to-all(f32[16,1,640]{2,1,0:T(1,128)S(1)} %broadcast_in_dim.15), channel_id=1, replica_groups=mesh['slab_0'=8,'slab_1'=4,'slab_2'=8,'slab_3'=2] {'slab_0','slab_3'}, dimensions={0} | all-to-all | bytes 81920 | tf_op jit(solution)/shard_map/all_to_all | solution.py:374
  49.1 2.8 %finish.1 = (f32[16,8,16,128]{3,2,1,0:T(8,128)}, f32[16,16]{1,0:T(8,128)}, f32[16,16]{1,0:T(8,128)}) custom-call(f32[80,128]{1,0:T(8,128)S(1)} %bitcast.3, bf16[256,1536]{1,0:T(8,128)(2,1)S(1)} %get-tuple-element.21.xf_ref, bf16[256,512]{1,0:T(8,128)(2,1)S(1)} %get-tuple-element.22.xe_ref, bf16[256,2048]{1,0:T(8,128)(2,1)S(1)} %get-tuple-element.16.xv_ref), custom_call_target="tpu_custom_call" | custom-call | flops 536870912 | bytes 3145728 | tf_op jit(solution)/shard_map/finish/pallas_call | solution.py:356
  (3 shorter events, 0.1 us)
Async XLA Ops:
  1.7 9.6 %copy-start = (f32[16,8,16,128]{3,2,1,0:T(8,128)S(1)}, f32[16,8,16,128]{3,2,1,0:T(8,128)}, u32[]{:S(2)}) copy-start(f32[16,8,16,128]{3,2,1,0:T(8,128)} %basis.1) | copy-start | bytes 3145732
  1.7 9.6 %copy-start.1 = (f32[16,8,16,128]{3,2,1,0:T(8,128)S(1)}, f32[16,8,16,128]{3,2,1,0:T(8,128)}, u32[]{:S(2)}) copy-start(f32[16,8,16,128]{3,2,1,0:T(8,128)} %companion.1) | copy-start | bytes 3145732
  1.7 11.5 %collective-permute-start = (f32[17,16,128]{2,1,0:T(8,128)S(1)}, f32[17,16,128]{2,1,0:T(8,128)S(1)}, u32[]{:S(2)}, u32[]{:S(2)}) collective-permute-start(f32[17,16,128]{2,1,0:T(8,128)S(1)} %hold.1.own0), channel_id=1, source_target_pairs={{1,2},{2,1},{3,4},{4,3},{5,6},{6,5},{7,8},{8,7},{9,10},{10,9},{11,... | collective-permute-start | bytes 417800 | tf_op jit(solution)/shard_map/ppermute | solution.py:384
  6.5 6.8 %collective-permute-start.1 = (f32[17,16,128]{2,1,0:T(8,128)S(1)}, f32[17,16,128]{2,1,0:T(8,128)S(1)}, u32[]{:S(2)}, u32[]{:S(2)}) collective-permute-start(f32[17,16,128]{2,1,0:T(8,128)S(1)} %get-tuple-element.18.own1), channel_id=1, source_target_pairs={{0,1},{1,0},{2,3},{3,2},{4,5},{5,4},{6,7},{7,6},{8,9},{9,8},{10,11... | collective-permute-start | bytes 417800 | tf_op jit(solution)/shard_map/ppermute | solution.py:385

commit v7 on v6

--- a/solution.py
+++ b/solution.py
@@ -385,8 +385,8 @@
     got1 = lax.ppermute(own[1], SLAB, pairs)
     xf, xv, edges, tiles = main(krylov_basis_block, fields, companion)
     xe, packed, xf = edge(core, edges, tiles, xv, own, (got0, got1), xf)
-    near = sent_to_all(packed.reshape(1, 640), ("slab_1", "slab_2")).sum(axis=0)
-    far = sent_to_all(near.reshape(1, 640), ("slab_0", "slab_3"))
+    near = sent_to_all(packed.reshape(1, 640), ("slab_2", "slab_3")).sum(axis=0)
+    far = sent_to_all(near.reshape(1, 640), ("slab_0", "slab_1"))
     new_block, projection, rfactor = finish(far.reshape(-1, 128), xf, xe, xv)
     return new_block, projection, rfactor
 

time: 52.2 us -> 50.7 us (0.971)
  blocking collectives: 35.1 us -> 33.7 us
    all_to_all x2, blocking collectives: 35.1 us -> 33.7 us  [sent_to_all(): lax.all_to_all(jnp.broadcast_to(x[None], (peers, *x.shape)), axes, 0, 0,...]
where the time goes in v7:
time: 50.7 us; the launch traced here: 50.5 us
  blocking collectives  33.7 us (66%)
  starting transfers between devices  9.55 us (19%)
  Pallas kernels  6.42 us (13%)
  between operations  0.75 us (1%)
    all_to_all x2, blocking collectives, sent_to_all(): lax.all_to_all(jnp.broadcast_to(x[None], (peers, *x.shape)), axes, 0, 0,...  33.7 us
    ppermute x1, starting transfers between devices, shards(): got1 = lax.ppermute(own[1], SLAB, pairs)  4.83 us
    ppermute x1, starting transfers between devices, shards(): got0 = lax.ppermute(own[0], SLAB, across)  4.71 us
    pallas_call x1, Pallas kernels, finish(): pl.pallas_call(finish_kernel, out_shape=(jax.ShapeDtypeStruct((NV, NX, NY...  2.84 us
    pallas_call x1, Pallas kernels, main(): pl.pallas_call(main_kernel, out_shape=(jax.ShapeDtypeStruct((256, 1536),...  1.88 us
    pallas_call x1, Pallas kernels, pack(): pl.pallas_call(pack_kernel, out_shape=(plane, plane, jax.ShapeDtypeStruct...  1.06 us
  transfers between devices with their start and end apart: 2, of which 0 were waited for; matrix products, arithmetic and copies ran while one was open for 0% of the time, Pallas kernels for 4%

profile of v7, /device:TPU:1, one launch (start us, length us, event | category | flops | bytes accessed | tf_op | source)
XLA Modules:
  0.0 50.5 jit_solution(11974300622766849830)
XLA Ops:
  0.6 1.1 %pack.1 = (f32[17,16,128]{2,1,0:T(8,128)S(1)}, f32[17,16,128]{2,1,0:T(8,128)S(1)}, f32[3,8,16,128]{3,2,1,0:T(8,128)S(1)}) custom-call(s32[1]{0:T(128)} %bitcast.core, f32[8]{0:T(128)} %dens_ref.1, f32[8]{0:T(128)} %stiff_ref.1, f32[8]{0:T(128)} %damp_ref.1, f32[16,8,16,128]{3,2,1,0:T(8,128)} %basis.1, s32[8,16,128]{2,1,0:T(8,128)} %region_ref.1), custom_call_target="tpu_custom_call" | custom-call | flops 262144 | bytes 524288 | tf_op jit(solution)/shard_map/pack/pallas_call | solution.py:59
  1.7 0.0 copy-start
  1.7 0.0 copy-start.1
  1.7 4.7 %collective-permute-start = (f32[17,16,128]{2,1,0:T(8,128)S(1)}, f32[17,16,128]{2,1,0:T(8,128)S(1)}, u32[]{:S(2)}, u32[]{:S(2)}) collective-permute-start(f32[17,16,128]{2,1,0:T(8,128)S(1)} %hold.1.own0), channel_id=1, source_target_pairs={{1,2},{2,1},{3,4},{4,3},{5,6},{6,5},{7,8},{8,7},{9,10},{10,9},{11,... | collective-permute-start | bytes 417800 | tf_op jit(solution)/shard_map/ppermute | solution.py:384
  6.5 4.8 %collective-permute-start.1 = (f32[17,16,128]{2,1,0:T(8,128)S(1)}, f32[17,16,128]{2,1,0:T(8,128)S(1)}, u32[]{:S(2)}, u32[]{:S(2)}) collective-permute-start(f32[17,16,128]{2,1,0:T(8,128)S(1)} %get-tuple-element.18.own1), channel_id=1, source_target_pairs={{0,1},{1,0},{2,3},{3,2},{4,5},{5,4},{6,7},{7,6},{8,9},{9,8},{10,11... | collective-permute-start | bytes 417800 | tf_op jit(solution)/shard_map/ppermute | solution.py:385
  11.3 0.0 copy-done
  11.3 0.0 copy-done.1
  11.3 1.9 %main.1 = (bf16[256,1536]{1,0:T(8,128)(2,1)S(1)}, bf16[256,2048]{1,0:T(8,128)(2,1)S(1)}, f32[2,16,16,128]{3,2,1,0:T(8,128)S(1)}, f32[48,128]{1,0:T(8,128)S(1)}) custom-call(f32[16,8,16,128]{3,2,1,0:T(8,128)S(1)} %copy-done, f32[3,8,16,128]{3,2,1,0:T(8,128)S(1)} %get-tuple-element.13.fields, f32[16,8,16,128]{3,2,1,0:T(8,128)S(1)} %copy-done.1), custom_call_target="tpu_custom_call" | custom-call | flops 268435456 | bytes 5242880 | tf_op jit(solution)/shard_map/main/pallas_call | solution.py:205
  13.2 0.0 collective-permute-done.got0
  13.2 0.0 collective-permute-done.1.got1
  13.2 0.6 %edge.1 = (bf16[256,512]{1,0:T(8,128)(2,1)S(1)}, f32[5,128]{1,0:T(8,128)S(1)}, bf16[256,1536]{1,0:T(8,128)(2,1)S(1)}) custom-call(s32[1]{0:T(128)} %bitcast.core, f32[2,16,16,128]{3,2,1,0:T(8,128)S(1)} %get-tuple-element.14.edge_ref, f32[48,128]{1,0:T(8,128)S(1)} %get-tuple-element.15.tiles_ref, ...), custom_call_target="tpu_custom_call", output_to_operand_aliasing={{2}: (8, {})} | custom-call | flops 134217728 | bytes 2097152 | tf_op jit(solution)/shard_map/edge/pallas_call | solution.py:253
  13.9 12.0 %all_to_all.10 = f32[16,1,640]{2,1,0:T(1,128)S(1)} all-to-all(f32[16,1,640]{2,1,0:T(1,128)S(1)} %broadcast_in_dim.14), channel_id=1, replica_groups=mesh['slab_0'=8,'slab_1'=4,'slab_2'=8,'slab_3'=2] {'slab_2','slab_3'}, dimensions={0} | all-to-all | bytes 81920 | tf_op jit(solution)/shard_map/all_to_all | solution.py:374
  26.0 21.6 %all_to_all.11 = f32[32,1,640]{2,1,0:T(1,128)S(1)} all-to-all(f32[32,1,640]{2,1,0:T(1,128)S(1)} %broadcast_in_dim.15), channel_id=1, replica_groups=mesh['slab_0'=8,'slab_1'=4,'slab_2'=8,'slab_3'=2] {'slab_0','slab_1'}, dimensions={0} | all-to-all | bytes 163840 | tf_op jit(solution)/shard_map/all_to_all | solution.py:374
  47.7 2.8 %finish.1 = (f32[16,8,16,128]{3,2,1,0:T(8,128)}, f32[16,16]{1,0:T(8,128)}, f32[16,16]{1,0:T(8,128)}) custom-call(f32[160,128]{1,0:T(8,128)S(1)} %bitcast.3, bf16[256,1536]{1,0:T(8,128)(2,1)S(1)} %get-tuple-element.21.xf_ref, bf16[256,512]{1,0:T(8,128)(2,1)S(1)} %get-tuple-element.22.xe_ref, bf16[256,2048]{1,0:T(8,128)(2,1)S(1)} %get-tuple-element.16.xv_ref), custom_call_target="tpu_custom_call" | custom-call | flops 536870912 | bytes 3145728 | tf_op jit(solution)/shard_map/finish/pallas_call | solution.py:356
  (4 shorter events, 0.1 us)
Async XLA Ops:
  1.7 9.6 %copy-start = (f32[16,8,16,128]{3,2,1,0:T(8,128)S(1)}, f32[16,8,16,128]{3,2,1,0:T(8,128)}, u32[]{:S(2)}) copy-start(f32[16,8,16,128]{3,2,1,0:T(8,128)} %basis.1) | copy-start | bytes 3145732
  1.7 9.6 %copy-start.1 = (f32[16,8,16,128]{3,2,1,0:T(8,128)S(1)}, f32[16,8,16,128]{3,2,1,0:T(8,128)}, u32[]{:S(2)}) copy-start(f32[16,8,16,128]{3,2,1,0:T(8,128)} %companion.1) | copy-start | bytes 3145732
  1.7 11.5 %collective-permute-start = (f32[17,16,128]{2,1,0:T(8,128)S(1)}, f32[17,16,128]{2,1,0:T(8,128)S(1)}, u32[]{:S(2)}, u32[]{:S(2)}) collective-permute-start(f32[17,16,128]{2,1,0:T(8,128)S(1)} %hold.1.own0), channel_id=1, source_target_pairs={{1,2},{2,1},{3,4},{4,3},{5,6},{6,5},{7,8},{8,7},{9,10},{10,9},{11,... | collective-permute-start | bytes 417800 | tf_op jit(solution)/shard_map/ppermute | solution.py:384
  6.5 6.8 %collective-permute-start.1 = (f32[17,16,128]{2,1,0:T(8,128)S(1)}, f32[17,16,128]{2,1,0:T(8,128)S(1)}, u32[]{:S(2)}, u32[]{:S(2)}) collective-permute-start(f32[17,16,128]{2,1,0:T(8,128)S(1)} %get-tuple-element.18.own1), channel_id=1, source_target_pairs={{0,1},{1,0},{2,3},{3,2},{4,5},{5,4},{6,7},{7,6},{8,9},{9,8},{10,11... | collective-permute-start | bytes 417800 | tf_op jit(solution)/shard_map/ppermute | solution.py:385
